TPU v7x, 512 devices: a whole 4x4x16 slice. The times are simulated.
512 devices in a mesh: tm: 64 (over z, x), sx: 4 (over y), sy: 2 (over core).
Axes of the slice: x: 4, y: 4, z: 16, core: 2. Of those that a mesh axis runs over, the one named last changes fastest.
Arguments:
- sources: float32 [128, 32, 32, 128], P('tm', 'sx', 'sy'), may hold values from -6 to 6
- forward_states: float32 [128, 32, 32, 128], P('tm', 'sx', 'sy'), may hold values from -6 to 6
- terminal: float32 [32, 32, 128], P('sx', 'sy'), may hold values from -6 to 6
- damping: float32 [32, 32, 128], P('sx', 'sy'), may hold values from 0.001 to 0.1
- contact_stiff: float32 [8], replicated, may hold values from 0.001 to 1
- regions: int32 [128, 4, 4], P('tm', 'sx', 'sy'), may hold values from 0 to 7
Outputs:
- adjoint: float32 [128, 32, 32, 128], P('tm', 'sx', 'sy')
- damping_grad: float32 [32, 32, 128], P('sx', 'sy')
Inputs may be any that keep to these rules, and one draw needn't show every extreme that they name: `regions`: region of a block of 8 x 8 columns of cells at a step.
All inputs are finite; a program needn't handle non-finite values.
Results may differ from a plain program's by a relative error of at most 0.0003.
Values sent between devices are 32-bit elements; how exact they have to be, the bound alone decides.
No kernel may reach another device: no remote copies, remote signals or barrier semaphores. Data moves between devices by JAX's collectives and lax.ppermute only.
A program may use at most 64 MiB of HBM per device.

v0:
```python
import jax
import jax.numpy as jnp
from jax import lax
from jax.sharding import PartitionSpec as P

SWEEPS = 4
REGIONS = 8
BLOCK_CELLS = 8


coupling = 0.5


def with_halo(array, sides, width):
    for axis, dim in sides:
        count, length = (lax.axis_size(axis), array.shape[dim])
        up = [(i, (i + 1) % count) for i in range(count - 1)]
        down = [(j, i) for i, j in up]
        last = lax.slice_in_dim(array, length - width, length, axis=dim)
        leading = lax.slice_in_dim(array, 0, width, axis=dim)
        before = lax.ppermute(last, axis, up)
        after = lax.ppermute(leading, axis, down)
        array = jnp.concatenate([before, array, after], axis=dim)
    return array


def passed_along(value, axis, steps):
    count = lax.axis_size(axis)
    leading, last = (max(0, -steps), min(count, count - steps))
    return lax.ppermute(value, axis, [(source, source + steps) for source in range(leading, last)])


def neighbours(field):
    extended = with_halo(field, (("sx", 0), ("sy", 1)), 1)
    padded = jnp.pad(extended, ((0, 0), (0, 0), (1, 1)))
    total = padded[2:, 1:-1, 1:-1] + padded[:-2, 1:-1, 1:-1]
    total = total + padded[1:-1, 2:, 1:-1] + padded[1:-1, :-2, 1:-1]
    total = total + padded[1:-1, 1:-1, 2:] + padded[1:-1, 1:-1, :-2]
    return total


def propagate(right, diagonal):
    field = right
    for sweep_index in range(SWEEPS):
        field = (right + coupling * neighbours(field)) / diagonal
    return field


def reaction(region_ids, contact_stiff, damping):
    labels = jnp.arange(REGIONS, dtype=jnp.int32)
    picked = jnp.sum(
        jnp.where(region_ids[:, :, None] == labels, contact_stiff, jnp.zeros_like(contact_stiff)),
        axis=2,
    )
    spread = jnp.repeat(jnp.repeat(picked, BLOCK_CELLS, axis=0), BLOCK_CELLS, axis=1)
    return spread[:, :, None] + damping


def shards(sources, forward_states, terminal, damping, contact_stiff, regions):
    steps_here = sources.shape[0]
    slab_index = lax.axis_index("tm")
    last_slab = slab_index == lax.axis_size("tm") - 1
    zeros_field = jnp.zeros_like(terminal)
    reactions = [
        reaction(regions[position], contact_stiff, damping) for position in range(steps_here)
    ]
    diagonals = [1.0 + reactions[position] + 6.0 * coupling for position in range(steps_here)]
    field = jnp.where(last_slab, terminal, zeros_field)
    for position in range(steps_here - 1, -1, -1):
        field = propagate(field, diagonals[position]) + sources[position]
    coarse_rhs = field
    factor = 1.0 / (1.0 + steps_here * reactions[0])

    def advance(iteration, value):
        return factor * passed_along(value, "tm", -1) + coarse_rhs

    corrected = lax.fori_loop(0, lax.axis_size("tm") - 1, advance, coarse_rhs)
    incoming = passed_along(corrected, "tm", -1)
    field = jnp.where(last_slab, terminal, incoming)
    layers = [corrected] * steps_here
    position = 1
    field = propagate(field, diagonals[position]) + sources[position]
    layers[position] = field
    adjoint = jnp.stack(layers)
    partial_grad = jnp.sum(adjoint * forward_states, axis=0)
    damping_grad = -lax.psum(partial_grad, "tm")
    return (adjoint, damping_grad)


def solution(mesh):
    in_specs = (
        P("tm", "sx", "sy", None),
        P("tm", "sx", "sy", None),
        P("sx", "sy", None),
        P("sx", "sy", None),
        P(),
        P("tm", "sx", "sy"),
    )
    out_specs = (P("tm", "sx", "sy", None), P("sx", "sy", None))
    return jax.shard_map(shards, mesh=mesh, in_specs=in_specs, out_specs=out_specs, check_vma=False)
```

profile of v0, /device:TPU:8, one launch (start us, length us, event | category | flops | bytes accessed | tf_op | source)
XLA Modules:
  0.0 1050.3 jit_solution(4107775764824397045)
XLA Ops:
  7.3 7.7 collective-permute-start.1
  119.7 539.4 %while.10 = (s32[]{:T(128)}, f32[8,16,128]{2,1,0:T(8,128)S(1)}, f32[8,16,128]{2,1,0:T(8,128)S(1)}, f32[8,16,128]{2,1,0:T(8,128)S(1)}, s32[]{:T(128)}) while((s32[]{:T(128)}, f32[8,16,128]{2,1,0:T(8,128)S(1)}, f32[8,16,128]{2,1,0:T(8,128)S(1)}, f32[8,16,128]{2,1,0:T(8,128)S(1)}, s32[]{:T(128)}) %tuple.50), condition=%wide.region_3.4_spmd, body=%wide.region_2.3_spmd.sunk | while | flops 32770 | bytes 524389 | solution.py:77
  165.6 7.5 collective-permute-done
  174.4 7.0 collective-permute-done
  182.8 7.2 collective-permute-done
  199.5 7.0 collective-permute-done
  207.8 7.0 collective-permute-done
  216.1 7.5 collective-permute-done
  224.8 7.2 collective-permute-done
  249.5 7.0 collective-permute-done
  257.8 7.0 collective-permute-done
  266.1 7.0 collective-permute-done
  274.4 7.5 collective-permute-done
  283.3 7.1 collective-permute-done
  308.2 7.0 collective-permute-done
  316.5 7.0 collective-permute-done
  324.8 7.5 collective-permute-done
  358.4 7.0 collective-permute-done
  366.7 7.0 collective-permute-done
  375.0 7.4 collective-permute-done
  383.6 7.1 collective-permute-done
  392.1 7.0 collective-permute-done
  433.1 7.0 collective-permute-done
  441.4 7.7 collective-permute-done
  450.4 8.3 collective-permute-done
  460.0 8.5 collective-permute-done
  469.8 8.2 collective-permute-done
  479.3 7.9 collective-permute-done
  488.5 7.9 collective-permute-done
  497.7 8.5 collective-permute-done
  507.5 7.9 collective-permute-done
  516.8 8.2 collective-permute-done
  526.3 9.0 collective-permute-done
  536.6 7.9 collective-permute-done
  545.8 8.4 collective-permute-done
  555.5 8.2 collective-permute-done
  565.1 8.1 collective-permute-done
  574.5 8.2 collective-permute-done
  584.0 8.6 collective-permute-done
  593.9 8.3 collective-permute-done
  603.5 8.3 collective-permute-done
  613.2 8.3 collective-permute-done
  622.8 7.9 collective-permute-done
  632.1 7.9 collective-permute-done
  641.3 8.5 collective-permute-done
  651.1 7.9 collective-permute-done
  660.3 8.2 collective-permute-done.33
  722.3 319.6 %all-reduce.14.cloned.1.call-done = f32[8,16,128]{2,1,0:T(8,128)} async-done(((f32[8,16,128]{2,1,0:T(8,128)}), f32[8,16,128]{2,1,0:T(8,128)}) %all-reduce.14.cloned.1.call-update) | async-done | bytes 65552 | tf_op jit(solution)/shard_map/psum | solution.py:86
  (314 shorter events, 360.1 us)
Async XLA Ops:
  7.2 1034.8 %all-reduce.14.cloned.1.call-start = ((), (), s32[]{:S(2)}) async-start(), calls=%async_computation | async-start | bytes 131072 | tf_op jit(solution)/shard_map/psum | solution.py:86
  7.3 9.7 collective-permute-start.1
  164.3 8.8 collective-permute-start
  173.1 8.3 collective-permute-start
  181.5 8.5 collective-permute-start
  198.2 8.3 collective-permute-start
  206.5 8.3 collective-permute-start
  214.8 8.8 collective-permute-start
  223.5 8.5 collective-permute-start
  248.2 8.3 collective-permute-start
  256.5 8.3 collective-permute-start
  264.8 8.3 collective-permute-start
  273.1 8.8 collective-permute-start
  282.0 8.4 collective-permute-start
  306.9 8.3 collective-permute-start
  315.2 8.3 collective-permute-start
  323.5 8.8 collective-permute-start
  357.1 8.3 collective-permute-start
  365.4 8.3 collective-permute-start
  373.7 8.7 collective-permute-start
  382.3 8.4 collective-permute-start
  390.8 8.3 collective-permute-start
  415.2 8.3 collective-permute-start
  431.8 8.3 collective-permute-start
  440.1 9.0 collective-permute-start
  449.1 9.6 collective-permute-start
  458.7 9.8 collective-permute-start
  468.5 9.5 collective-permute-start
  478.0 9.2 collective-permute-start
  487.2 9.2 collective-permute-start
  496.4 9.8 collective-permute-start
  506.2 9.2 collective-permute-start
  515.5 9.5 collective-permute-start
  525.0 10.3 collective-permute-start
  535.3 9.2 collective-permute-start
  544.5 9.7 collective-permute-start
  554.2 9.5 collective-permute-start
  563.8 9.4 collective-permute-start
  573.2 9.5 collective-permute-start
  582.7 9.9 collective-permute-start
  592.6 9.6 collective-permute-start
  602.2 9.6 collective-permute-start
  611.9 9.6 collective-permute-start
  621.5 9.2 collective-permute-start
  630.8 9.2 collective-permute-start
  640.0 9.8 collective-permute-start
  649.8 9.2 collective-permute-start
  659.0 9.5 collective-permute-start.33
  (71 other events, 385.5 us)
Sparse Core Ops, SparseCore 0:
  722.4 319.4 all-reduce.13
where the time goes:
time: 1050 us
  waiting for transfers between devices  815 us (78%)
  starting transfers between devices  209 us (20%)
  between operations  15 us (1%)
    ppermute x64, waiting for transfers between devices, passed_along(): lax.ppermute(value, axis, [(source, source + steps) for source in range(l...  464 us
    psum x1, waiting for transfers between devices, shards(): damping_grad = -lax.psum(partial_grad, 'tm')  320 us
    ppermute x64, starting transfers between devices, passed_along(): lax.ppermute(value, axis, [(source, source + steps) for source in range(l...  82.7 us
    ppermute x24, starting transfers between devices, with_halo(): before = lax.ppermute(last, axis, up)  81.6 us
    ppermute x24, starting transfers between devices, with_halo(): after = lax.ppermute(leading, axis, down)  44.4 us
    ppermute x24, waiting for transfers between devices, with_halo(): before = lax.ppermute(last, axis, up)  28.2 us
  transfers between devices with their start and end apart: 113, of which 88 were waited for; matrix products, arithmetic and copies ran while one was open for 0% of the time, Pallas kernels for 0%

commit v1 on v0

v1 whole, which is shorter than its diff:
```python
import functools
import jax
import jax.numpy as jnp
from jax import lax
from jax.experimental import pallas as pl
from jax.experimental.pallas import tpu as pltpu
from jax.sharding import PartitionSpec as P

F32 = jnp.float32
COUPLING = 0.5
CENTRE = 1.0 + 6.0 * COUPLING

NZ, NX4, ND = 16, 4, 8
X_GROUPS = [[z * NX4 + x for x in range(NX4)] for z in range(NZ)]
Z_GROUPS = [[z * NX4 + x for z in range(NZ)] for x in range(NX4)]

T_OWN = 16
SRC1 = (0, 32, 8)
DAMP = (32, 40, 12)
TERM = (72, 40, 12)
SRC0 = (112, 24, 4)
REACT = 136
ROWS1 = 144


def xy_neighbours(f):
    sub = lax.broadcasted_iota(jnp.int32, f.shape, 1)
    lane = lax.broadcasted_iota(jnp.int32, f.shape, 2)
    yl = lane % 16
    xp = pltpu.roll(f, 112, 2)
    xm = pltpu.roll(f, 16, 2)
    xpc = pltpu.roll(xp, 6, 1)
    xmc = pltpu.roll(xm, 2, 1)
    zero = jnp.zeros_like(f)
    total = jnp.where(lane < 112, xp, jnp.where(sub < 6, xpc, zero))
    total = total + jnp.where(lane >= 16, xm, jnp.where(sub >= 2, xmc, zero))
    yp = pltpu.roll(f, 127, 2)
    ym = pltpu.roll(f, 1, 2)
    even = (sub % 2) == 0
    ypc = pltpu.roll(pltpu.roll(f, 15, 2), 7, 1)
    ymc = pltpu.roll(pltpu.roll(f, 113, 2), 1, 1)
    total = total + jnp.where(yl < 15, yp, jnp.where(even, ypc, zero))
    total = total + jnp.where(yl > 0, ym, jnp.where(even, zero, ymc))
    return total


def phi(b, inv):
    n = b.shape[0]
    x = b
    for s in range(1, 5):
        nb = x[2:] + x[:-2] + xy_neighbours(x[1:-1])
        rows = slice(s, n - s)
        x = (b[rows] + COUPLING * nb) * inv[s - 1 : n - s - 1]
    return x


def row_mask(rows, halo, d):
    t = lax.broadcasted_iota(jnp.int32, (rows, 8, 128), 0) + d * T_OWN - halo
    return (t >= 0) & (t < 128)


def pack_kernel(stiff_ref, reg_ref, src_ref, damp_ref, term_ref, out_ref, pad):
    pad[...] = jnp.zeros_like(pad)

    def put(value, spec):
        off, rows, halo = spec
        pad[halo : halo + 128, :] = value.reshape(128, 128).T
        pad[halo + 128 : 2 * halo + 128, :] = jnp.zeros((halo, 128), F32)
        pad[0:halo, :] = jnp.zeros((halo, 128), F32)
        for d in range(ND):
            out_ref[d, off : off + rows, :] = pad[T_OWN * d : T_OWN * d + rows, :]

    put(src_ref[1], SRC1)
    put(damp_ref[...], DAMP)
    put(term_ref[...], TERM)
    put(src_ref[0], SRC0)
    yl = lax.broadcasted_iota(jnp.int32, (1, 128), 1) % 16
    rows = []
    for k in (1, 0):
        r0 = stiff_ref[reg_ref[2 * k]]
        r1 = stiff_ref[reg_ref[2 * k + 1]]
        rows.append(jnp.where(yl < 8, r0, r1).astype(F32))
    tail = jnp.concatenate(rows + [jnp.zeros((6, 128), F32)], axis=0)
    for d in range(ND):
        out_ref[d, REACT : REACT + 8, :] = tail


def spread(scr, recv_ref, off, rows, base=0):
    for s in range(ND):
        scr[pl.ds(s, rows, stride=8), :] = recv_ref[s, off : off + rows, :]
    return scr[0 : rows * 8, :].reshape(rows, 8, 128)


def first_kernel(idx_ref, recv_ref, out_ref, inv_ref, scr):
    d = idx_ref[2]
    last = (idx_ref[0] == NZ - 1) & (idx_ref[1] == NX4 - 1)
    react1 = recv_ref[:, REACT, :]
    react0 = recv_ref[:, REACT + 1, :]
    damp = spread(scr, recv_ref, DAMP[0], DAMP[1])
    inside = row_mask(40, 12, d)
    zero = jnp.zeros((40, 8, 128), F32)
    inv1 = jnp.where(inside, 1.0 / (CENTRE + (react1[None] + damp)), zero)
    inv0 = jnp.where(inside, 1.0 / (CENTRE + (react0[None] + damp)), zero)
    inv_ref[...] = inv1[9:31]
    term = spread(scr, recv_ref, TERM[0], TERM[1])
    term = jnp.where(last, term, zero)
    v = phi(term, inv1[1:39])
    v = v + spread(scr, recv_ref, SRC1[0], SRC1[1])
    rhs = phi(v, inv0[5:35])
    rhs = rhs + spread(scr, recv_ref, SRC0[0], SRC0[1])
    scr[0 : 24 * 8, :] = rhs.reshape(24 * 8, 128)
    for s in range(ND):
        q, sub = s // 2, s % 2
        out_ref[q, 24 * sub : 24 * sub + 24, :] = scr[pl.ds(s, 24, stride=8), :]
        out_ref[q, 48 + sub : 49 + sub, :] = recv_ref[s, REACT + 1 : REACT + 2, :]
    for q in range(NX4):
        out_ref[q, 50:56, :] = jnp.zeros((6, 128), F32)


def quarter_damp(idx_ref, recv_ref):
    x = idx_ref[1]
    rows = slice(DAMP[0] + 8, DAMP[0] + 32)
    return jnp.concatenate([recv_ref[2 * x, rows, :], recv_ref[2 * x + 1, rows, :]], axis=0)


def per_pair(r0, r1):
    return jnp.concatenate([jnp.broadcast_to(r0, (24, 128)), jnp.broadcast_to(r1, (24, 128))], axis=0)


def compose_kernel(idx_ref, recv1_ref, recv_ref, out_ref):
    damp = quarter_damp(idx_ref, recv1_ref)
    carry = recv_ref[3, 0:48, :]
    for x in (2, 1, 0):
        react = per_pair(recv_ref[x, 48:49, :], recv_ref[x, 49:50, :])
        carry = carry / (1.0 + 2.0 * (react + damp)) + recv_ref[x, 0:48, :]
    tail = jnp.concatenate([recv_ref[x, 48:50, :] for x in range(NX4)], axis=0)
    for z in range(NZ):
        out_ref[z, 0:48, :] = carry
        out_ref[z, 48:56, :] = tail


def scan_kernel(idx_ref, recv1_ref, recv2_ref, recv_ref, out_ref):
    z = idx_ref[0]
    damp = quarter_damp(idx_ref, recv1_ref)

    def step(i, carry):
        zz = NZ - 1 - i
        den = None
        for x in range(NX4):
            react = per_pair(recv_ref[zz, pl.ds(48 + 2 * x, 1), :], recv_ref[zz, pl.ds(49 + 2 * x, 1), :])
            term = 1.0 + 2.0 * (react + damp)
            den = term if den is None else den * term
        return carry / den + recv_ref[zz, 0:48, :]

    carry = lax.fori_loop(0, NZ - 1 - z, step, jnp.zeros((48, 128), F32))
    for x in (3, 2, 1, 0):
        react = per_pair(recv2_ref[x, 48:49, :], recv2_ref[x, 49:50, :])
        own = carry / (1.0 + 2.0 * (react + damp)) + recv2_ref[x, 0:48, :]
        out_ref[x, 0:48, :] = carry
        out_ref[x, 48:64, :] = own[4:20]
        out_ref[x, 64:80, :] = own[28:44]
        carry = own


def final_kernel(idx_ref, recv1_ref, inv_ref, recv_ref, out_ref, scr):
    last = (idx_ref[0] == NZ - 1) & (idx_ref[1] == NX4 - 1)
    for s in range(ND):
        q, sub = s // 2, s % 2
        incoming = recv_ref[q, 24 * sub : 24 * sub + 24, :]
        term = recv1_ref[s, TERM[0] + 8 : TERM[0] + 32, :]
        scr[pl.ds(s, 24, stride=8), :] = jnp.where(last, term, incoming)
        out_ref[s, 0:16, :] = recv_ref[q, 48 + 16 * sub : 64 + 16 * sub, :]
    w = phi(scr[...].reshape(24, 8, 128), inv_ref[...])
    scr[0:128, :] = w.reshape(128, 128)
    for s in range(ND):
        out_ref[s, 16:32, :] = scr[pl.ds(s, 16, stride=8), :] + recv1_ref[s, SRC1[0] + 8 : SRC1[0] + 24, :]


def unpack_kernel(recv_ref, state_ref, adj_ref, part_ref):
    total = None
    for k in range(2):
        rows = jnp.concatenate([recv_ref[s, 16 * k : 16 * k + 16, :] for s in range(ND)], axis=0)
        value = rows.T
        adj_ref[k] = value.reshape(8, 16, 128)
        prod = value * state_ref[k].reshape(128, 128)
        total = prod if total is None else total + prod
    part_ref[...] = (-total).reshape(4, 32, 128)


def sum_kernel(copies, recv_ref, out_ref):
    total = recv_ref[0]
    for i in range(1, recv_ref.shape[0]):
        total = total + recv_ref[i]
    for i in range(copies):
        out_ref[i] = total


VM = pl.BlockSpec(memory_space=pltpu.VMEM)
SM = pl.BlockSpec(memory_space=pltpu.SMEM)
INTERPRET = False


def call(kernel, outs, in_specs, scratch=(), name=None):
    shapes = [jax.ShapeDtypeStruct(s, F32) for s in outs]
    single = len(shapes) == 1
    return pl.pallas_call(
        kernel,
        out_shape=shapes[0] if single else shapes,
        in_specs=in_specs,
        out_specs=VM if single else [VM] * len(shapes),
        scratch_shapes=list(scratch),
        name=name,
        interpret=INTERPRET,
    )


def shards(sources, forward_states, terminal, damping, contact_stiff, regions):
    tm = lax.axis_index("tm")
    d = lax.axis_index("sx") * 2 + lax.axis_index("sy")
    idx = jnp.stack([tm // NX4, tm % NX4, d]).astype(jnp.int32)

    def over_space(v):
        return lax.all_to_all(v, ("sx", "sy"), 0, 0, tiled=True)

    def over_x(v):
        return lax.all_to_all(v, "tm", 0, 0, tiled=True, axis_index_groups=X_GROUPS)

    def over_z(v):
        return lax.all_to_all(v, "tm", 0, 0, tiled=True, axis_index_groups=Z_GROUPS)

    send1 = call(pack_kernel, [(ND, ROWS1, 128)], [SM, SM, VM, VM, VM], [pltpu.VMEM((152, 128), F32)], "pack")(
        contact_stiff, regions.reshape(4), sources, damping, terminal
    )
    recv1 = over_space(send1)
    send2, inv1 = call(first_kernel, [(NX4, 56, 128), (22, 8, 128)], [SM, VM], [pltpu.VMEM((320, 128), F32)], "first")(
        idx, recv1
    )
    recv2 = over_x(send2)
    sendz = call(compose_kernel, [(NZ, 56, 128)], [SM, VM, VM], name="compose")(idx, recv1, recv2)
    recvz = over_z(sendz)
    send3 = call(scan_kernel, [(NX4, 80, 128)], [SM, VM, VM, VM], name="scan")(idx, recv1, recv2, recvz)
    recv3 = over_x(send3)
    send4 = call(final_kernel, [(ND, 32, 128)], [SM, VM, VM, VM], [pltpu.VMEM((192, 128), F32)], "final")(
        idx, recv1, inv1, recv3
    )
    recv4 = over_space(send4)
    adjoint, part = call(unpack_kernel, [(2, 8, 16, 128), (4, 32, 128)], [VM, VM], name="unpack")(recv4, forward_states)
    part = over_x(part)
    part = call(functools.partial(sum_kernel, NZ), [(NZ, 32, 128)], [VM], name="sum_x")(part)
    part = over_z(part)
    part = call(functools.partial(sum_kernel, NX4), [(NX4, 32, 128)], [VM], name="sum_z")(part)
    grad = over_x(part)
    return adjoint, grad.reshape(8, 16, 128)


def solution(mesh):
    in_specs = (
        P("tm", "sx", "sy", None),
        P("tm", "sx", "sy", None),
        P("sx", "sy", None),
        P("sx", "sy", None),
        P(),
        P("tm", "sx", "sy"),
    )
    out_specs = (P("tm", "sx", "sy", None), P("sx", "sy", None))
    return jax.shard_map(shards, mesh=mesh, in_specs=in_specs, out_specs=out_specs, check_vma=False)
```

time: 1050 us -> 151 us (0.14)
  the two profiles are of different devices: /device:TPU:8 before, /device:TPU:32 now
where the time goes in v1:
time: 151 us; the launch traced here: 150 us
  blocking collectives  113 us (75%)
  Pallas kernels  17.5 us (12%)
  waiting for transfers between devices  10.4 us (7%)
  starting transfers between devices  4.47 us (3%)
  local copies, waits for them, and re-layouts  2.71 us (2%)
    all_to_all x2, blocking collectives, over_z(): return lax.all_to_all(v, 'tm', 0, 0, tiled=True, axis_index_groups=Z_GROUPS)  63.9 us
    all_to_all x4, blocking collectives, over_x(): return lax.all_to_all(v, 'tm', 0, 0, tiled=True, axis_index_groups=X_GROUPS)  38.9 us
    all_to_all x1, waiting for transfers between devices, over_space(): return lax.all_to_all(v, ('sx', 'sy'), 0, 0, tiled=True)  10.4 us
    all_to_all x1, blocking collectives, over_space(): return lax.all_to_all(v, ('sx', 'sy'), 0, 0, tiled=True)  10.1 us
    all_to_all x1, starting transfers between devices, over_space(): return lax.all_to_all(v, ('sx', 'sy'), 0, 0, tiled=True)  4.47 us
    pallas_call x1, Pallas kernels, shards(): call(first_kernel, [(NX4, 56, 128), (22, 8, 128)], [SM, VM], [pltpu.VMEM(...  3.91 us
  transfers between devices with their start and end apart: 1, of which 1 were waited for; matrix products, arithmetic and copies ran while one was open for 0% of the time, Pallas kernels for 0%

profile of v1, /device:TPU:32, one launch (start us, length us, event | category | flops | bytes accessed | tf_op | source)
XLA Modules:
  0.0 150.0 jit_solution(3445260079448218918)
XLA Ops:
  0.6 0.0 copy-start.1
  0.6 0.5 broadcast.5
  1.2 0.2 copy-done.1
  1.3 0.7 reduce.3
  2.0 0.6 reshape.10.reg_ref
  2.6 1.9 %pack.1 = f32[8,144,128]{2,1,0:T(8,128)} custom-call(f32[8]{0:T(128)} %stiff_ref.1, s32[4]{0:T(128)} %reshape.10.reg_ref, f32[2,8,16,128]{3,2,1,0:T(8,128)} %src_ref.1, f32[8,16,128]{2,1,0:T(8,128)} %damp_ref.1, f32[8,16,128]{2,1,0:T(8,128)} %term_ref.1), custom_call_target="tpu_custom_call" | custom-call | tf_op jit(solution)/shard_map/pack/pallas_call | solution.py:231
  4.5 4.5 %all-to-all-start = ((f32[8,144,128]{2,1,0:T(8,128)}), f32[8,144,128]{2,1,0:T(8,128)S(1)}, u32[]{:S(2)}, u32[]{:S(2)}) async-start(f32[8,144,128]{2,1,0:T(8,128)} %pack.1), calls=%async_computation | async-start | bytes 1179648 | tf_op jit(solution)/shard_map/all_to_all | solution.py:223
  9.0 0.6 pad_add_fusion.idx_ref
  9.6 10.4 %all-to-all-done.recv_ref.recv1_ref = f32[8,144,128]{2,1,0:T(8,128)S(1)} async-done(((f32[8,144,128]{2,1,0:T(8,128)}), f32[8,144,128]{2,1,0:T(8,128)S(1)}, u32[]{:S(2)}, u32[]{:S(2)}) %all-to-all-start) | async-done | bytes 589856 | tf_op jit(solution)/shard_map/all_to_all | solution.py:223
  20.0 0.0 copy-start
  20.0 0.8 copy-done
  20.9 3.9 %first.1 = (f32[4,56,128]{2,1,0:T(8,128)}, f32[22,8,128]{2,1,0:T(8,128)}) custom-call(s32[3]{0:T(128)} %pad_add_fusion.idx_ref, f32[8,144,128]{2,1,0:T(8,128)} %copy-done), custom_call_target="tpu_custom_call" | custom-call | tf_op jit(solution)/shard_map/first/pallas_call | solution.py:235
  24.8 10.3 %all_to_all.40.recv_ref.recv2_ref = f32[4,56,128]{2,1,0:T(8,128)} all-to-all(f32[4,56,128]{2,1,0:T(8,128)} %get-tuple-element.7), channel_id=1, replica_groups={{0,8,16,24},{32,40,48,56},{64,72,80,88},{96,104,112,120},{128,136,144,1..., dimensions={0} | all-to-all | bytes 229376 | tf_op jit(solution)/shard_map/all_to_all | solution.py:226
  35.0 1.9 %compose.1 = f32[16,56,128]{2,1,0:T(8,128)} custom-call(s32[3]{0:T(128)} %pad_add_fusion.idx_ref, f32[8,144,128]{2,1,0:T(8,128)} %copy-done, f32[4,56,128]{2,1,0:T(8,128)} %all_to_all.40.recv_ref.recv2_ref), custom_call_target="tpu_custom_call" | custom-call | tf_op jit(solution)/shard_map/compose/pallas_call | solution.py:239
  37.0 39.2 %all_to_all.41.recv_ref = f32[16,56,128]{2,1,0:T(8,128)} all-to-all(f32[16,56,128]{2,1,0:T(8,128)} %compose.1), channel_id=1, replica_groups={{0,32,64,96,128,160,192,224,256,288,320,352,384,416,448,480},{8,40,72,1..., dimensions={0} | all-to-all | bytes 917504 | tf_op jit(solution)/shard_map/all_to_all | solution.py:229
  76.2 2.3 %scan.1 = f32[4,80,128]{2,1,0:T(8,128)} custom-call(s32[3]{0:T(128)} %pad_add_fusion.idx_ref, f32[8,144,128]{2,1,0:T(8,128)} %copy-done, f32[4,56,128]{2,1,0:T(8,128)} %all_to_all.40.recv_ref.recv2_ref, f32[16,56,128]{2,1,0:T(8,128)} %all_to_all.41.recv_ref), custom_call_target="tpu_custom_call" | custom-call | tf_op jit(solution)/shard_map/scan/pallas_call | solution.py:241
  78.5 10.2 %all_to_all.42.recv_ref = f32[4,80,128]{2,1,0:T(8,128)} all-to-all(f32[4,80,128]{2,1,0:T(8,128)} %scan.1), channel_id=1, replica_groups={{0,8,16,24},{32,40,48,56},{64,72,80,88},{96,104,112,120},{128,136,144,1..., dimensions={0} | all-to-all | bytes 327680 | tf_op jit(solution)/shard_map/all_to_all | solution.py:226
  88.7 2.6 %final.1 = f32[8,32,128]{2,1,0:T(8,128)} custom-call(s32[3]{0:T(128)} %pad_add_fusion.idx_ref, f32[8,144,128]{2,1,0:T(8,128)} %copy-done, f32[22,8,128]{2,1,0:T(8,128)} %get-tuple-element.6.inv_ref, f32[4,80,128]{2,1,0:T(8,128)} %all_to_all.42.recv_ref), custom_call_target="tpu_custom_call" | custom-call | tf_op jit(solution)/shard_map/final/pallas_call | solution.py:243
  91.2 10.1 %all_to_all.43.recv_ref = f32[8,32,128]{2,1,0:T(8,128)} all-to-all(f32[8,32,128]{2,1,0:T(8,128)} %final.1), channel_id=1, replica_groups=mesh['tm'=64,'sx'=4,'sy'=2] {'sx','sy'}, dimensions={0} | all-to-all | bytes 262144 | tf_op jit(solution)/shard_map/all_to_all | solution.py:223
  101.4 1.7 %unpack.1 = (f32[2,8,16,128]{3,2,1,0:T(8,128)}, f32[4,32,128]{2,1,0:T(8,128)}) custom-call(f32[8,32,128]{2,1,0:T(8,128)} %all_to_all.43.recv_ref, f32[2,8,16,128]{3,2,1,0:T(8,128)} %state_ref.1), custom_call_target="tpu_custom_call" | custom-call | tf_op jit(solution)/shard_map/unpack/pallas_call | solution.py:247
  103.1 9.6 %all_to_all.44.recv_ref = f32[4,32,128]{2,1,0:T(8,128)} all-to-all(f32[4,32,128]{2,1,0:T(8,128)} %get-tuple-element.9), channel_id=1, replica_groups={{0,8,16,24},{32,40,48,56},{64,72,80,88},{96,104,112,120},{128,136,144,1..., dimensions={0} | all-to-all | bytes 131072 | tf_op jit(solution)/shard_map/all_to_all | solution.py:226
  112.7 1.6 %sum_x.1 = f32[16,32,128]{2,1,0:T(8,128)} custom-call(f32[4,32,128]{2,1,0:T(8,128)} %all_to_all.44.recv_ref), custom_call_target="tpu_custom_call" | custom-call | tf_op jit(solution)/shard_map/sum_x/pallas_call | solution.py:249
  114.2 24.7 %all_to_all.45.recv_ref = f32[16,32,128]{2,1,0:T(8,128)} all-to-all(f32[16,32,128]{2,1,0:T(8,128)} %sum_x.1), channel_id=1, replica_groups={{0,32,64,96,128,160,192,224,256,288,320,352,384,416,448,480},{8,40,72,1..., dimensions={0} | all-to-all | bytes 524288 | tf_op jit(solution)/shard_map/all_to_all | solution.py:229
  138.9 1.6 %sum_z.1 = f32[4,32,128]{2,1,0:T(8,128)} custom-call(f32[16,32,128]{2,1,0:T(8,128)} %all_to_all.45.recv_ref), custom_call_target="tpu_custom_call" | custom-call | tf_op jit(solution)/shard_map/sum_z/pallas_call | solution.py:251
  140.5 8.9 %all_to_all.46 = f32[4,32,128]{2,1,0:T(8,128)S(1)} all-to-all(f32[4,32,128]{2,1,0:T(8,128)} %sum_z.1), channel_id=1, replica_groups={{0,8,16,24},{32,40,48,56},{64,72,80,88},{96,104,112,120},{128,136,144,1..., dimensions={0} | all-to-all | bytes 131072 | tf_op jit(solution)/shard_map/all_to_all | solution.py:226
  149.4 0.6 copy.9
Async XLA Ops:
  0.6 0.7 copy-start.1
  4.5 15.5 %all-to-all-start = ((f32[8,144,128]{2,1,0:T(8,128)}), f32[8,144,128]{2,1,0:T(8,128)S(1)}, u32[]{:S(2)}, u32[]{:S(2)}) async-start(f32[8,144,128]{2,1,0:T(8,128)} %pack.1), calls=%async_computation | async-start | bytes 1179648 | tf_op jit(solution)/shard_map/all_to_all | solution.py:223
  20.0 0.8 copy-start

commit v2 on v1

v2 whole, which is shorter than its diff:
```python
import jax
import jax.numpy as jnp
from jax import lax
from jax.experimental import pallas as pl
from jax.experimental.pallas import tpu as pltpu
from jax.sharding import PartitionSpec as P

F32 = jnp.float32
COUPLING = 0.5
CENTRE = 1.0 + 6.0 * COUPLING

NZ, NX4, ND = 16, 4, 8

T_OWN = 16
SRC1 = (0, 32, 8)
DAMP = (32, 40, 12)
TERM = (72, 40, 12)
SRC0 = (112, 24, 4)
REACT = 136
ROWS1 = 144


def xy_neighbours(f):
    sub = lax.broadcasted_iota(jnp.int32, f.shape, 1)
    lane = lax.broadcasted_iota(jnp.int32, f.shape, 2)
    yl = lane % 16
    xp = pltpu.roll(f, 112, 2)
    xm = pltpu.roll(f, 16, 2)
    xpc = pltpu.roll(xp, 6, 1)
    xmc = pltpu.roll(xm, 2, 1)
    zero = jnp.zeros_like(f)
    total = jnp.where(lane < 112, xp, jnp.where(sub < 6, xpc, zero))
    total = total + jnp.where(lane >= 16, xm, jnp.where(sub >= 2, xmc, zero))
    yp = pltpu.roll(f, 127, 2)
    ym = pltpu.roll(f, 1, 2)
    even = (sub % 2) == 0
    ypc = pltpu.roll(pltpu.roll(f, 15, 2), 7, 1)
    ymc = pltpu.roll(pltpu.roll(f, 113, 2), 1, 1)
    total = total + jnp.where(yl < 15, yp, jnp.where(even, ypc, zero))
    total = total + jnp.where(yl > 0, ym, jnp.where(even, zero, ymc))
    return total


def phi(b, inv):
    n = b.shape[0]
    x = b
    for s in range(1, 5):
        nb = x[2:] + x[:-2] + xy_neighbours(x[1:-1])
        rows = slice(s, n - s)
        x = (b[rows] + COUPLING * nb) * inv[s - 1 : n - s - 1]
    return x


def row_mask(rows, halo, d):
    t = lax.broadcasted_iota(jnp.int32, (rows, 8, 128), 0) + d * T_OWN - halo
    return (t >= 0) & (t < 128)


def pack_kernel(stiff_ref, reg_ref, src_ref, damp_ref, term_ref, out_ref, pad):
    def put(value, spec):
        off, rows, halo = spec
        pad[halo : halo + 128, :] = value.reshape(128, 128).T
        pad[halo + 128 : 2 * halo + 128, :] = jnp.zeros((halo, 128), F32)
        pad[0:halo, :] = jnp.zeros((halo, 128), F32)
        for d in range(ND):
            out_ref[d, off : off + rows, :] = pad[T_OWN * d : T_OWN * d + rows, :]

    put(src_ref[1], SRC1)
    put(damp_ref[...], DAMP)
    put(term_ref[...], TERM)
    put(src_ref[0], SRC0)
    yl = lax.broadcasted_iota(jnp.int32, (8, 128), 1) % 16
    row = lax.broadcasted_iota(jnp.int32, (8, 128), 0)
    react = []
    for k in range(2):
        react.append(jnp.where(yl < 8, stiff_ref[reg_ref[k, 0, 0]], stiff_ref[reg_ref[k, 0, 1]]))
    tail = jnp.where(row == 0, react[1], react[0])
    for d in range(ND):
        out_ref[d, REACT : REACT + 8, :] = tail


def spread(scr, recv_ref, off, rows):
    for s in range(ND):
        scr[pl.ds(s, rows, stride=8), :] = recv_ref[s, off : off + rows, :]
    return scr[0 : rows * 8, :].reshape(rows, 8, 128)


def first_kernel(recv_ref, out_ref, inv_ref, rhs_ref, fac_ref, scr_d, scr_t, scr1, scr0):
    d = lax.axis_index("sx") * 2 + lax.axis_index("sy")
    last = lax.axis_index("tm") == NZ * NX4 - 1
    react1 = recv_ref[:, REACT, :]
    react0 = recv_ref[:, REACT + 1, :]
    damp = spread(scr_d, recv_ref, DAMP[0], DAMP[1])
    inside = row_mask(40, 12, d)
    zero = jnp.zeros((40, 8, 128), F32)
    inv1 = jnp.where(inside, 1.0 / (CENTRE + (react1[None] + damp)), zero)
    inv0 = jnp.where(inside, 1.0 / (CENTRE + (react0[None] + damp)), zero)
    inv_ref[...] = inv1[9:31]
    fac_ref[...] = 1.0 / (1.0 + 2.0 * (react0[None] + damp[12:28]))
    term = spread(scr_t, recv_ref, TERM[0], TERM[1])
    term = jnp.where(last, term, zero)
    v = phi(term, inv1[1:39])
    v = v + spread(scr1, recv_ref, SRC1[0], SRC1[1])
    rhs = phi(v, inv0[5:35])
    rhs = rhs + spread(scr0, recv_ref, SRC0[0], SRC0[1])
    rhs_ref[...] = rhs[4:20]
    scr_t[0 : 24 * 8, :] = rhs.reshape(24 * 8, 128)
    for s in range(ND):
        for i in range(3):
            out_ref[pl.ds(32 * s + i, 8, stride=4), :] = scr_t[pl.ds(64 * i + s, 8, stride=8), :]
        out_ref[pl.ds(32 * s + 3, 8, stride=4), :] = jnp.broadcast_to(recv_ref[s, REACT + 1 : REACT + 2, :], (8, 128))


def scan_kernel(recv1_ref, recv_ref, out_ref):
    t = lax.axis_index("tm")
    s, g = t // 8, t % 8
    sub = lax.broadcasted_iota(jnp.int32, (8, 128), 0)
    low = sub < 4
    damp = jnp.zeros((8, 128), F32)
    for i in range(3):
        row = recv1_ref[s, pl.ds(DAMP[0] + 8 + 8 * i + g, 1), :]
        damp = jnp.where(sub % 4 == i, row, damp)
    carry = jnp.zeros((8, 128), F32)
    for m in range(31, -1, -1):
        tile = recv_ref[8 * m : 8 * m + 8, :]
        react = jnp.where(low, tile[3:4], tile[7:8])
        fac = 1.0 / (1.0 + 2.0 * (react + damp))
        fac_hi = pltpu.roll(fac, 4, 0)
        rhs_hi = pltpu.roll(tile, 4, 0)
        next_lo = fac_hi * carry + rhs_hi
        out_ref[8 * m : 8 * m + 8, :] = jnp.where(low, next_lo, pltpu.roll(carry, 4, 0))
        carry = (fac * fac_hi) * carry + (fac * rhs_hi + tile)


def final_kernel(recv1_ref, inv_ref, rhs_ref, fac_ref, recv_ref, out_ref, scr):
    last = lax.axis_index("tm") == NZ * NX4 - 1
    for s in range(ND):
        for i in range(3):
            scr[pl.ds(64 * i + s, 8, stride=8), :] = recv_ref[pl.ds(32 * s + i, 8, stride=4), :]
    incoming = scr[...].reshape(24, 8, 128)
    own = fac_ref[...] * incoming[4:20] + rhs_ref[...]
    scr[0:128, :] = own.reshape(128, 128)
    for s in range(ND):
        out_ref[s, 0:16, :] = scr[pl.ds(s, 16, stride=8), :]
    for s in range(ND):
        scr[pl.ds(s, 24, stride=8), :] = recv1_ref[s, TERM[0] + 8 : TERM[0] + 32, :]
    w = phi(jnp.where(last, scr[...].reshape(24, 8, 128), incoming), inv_ref[...])
    scr[0:128, :] = w.reshape(128, 128)
    for s in range(ND):
        out_ref[s, 16:32, :] = scr[pl.ds(s, 16, stride=8), :] + recv1_ref[s, SRC1[0] + 8 : SRC1[0] + 24, :]


def unpack_kernel(recv_ref, state_ref, adj_ref, part_ref):
    total = None
    for k in range(2):
        rows = jnp.concatenate([recv_ref[s, 16 * k : 16 * k + 16, :] for s in range(ND)], axis=0)
        value = rows.T
        adj_ref[k] = value.reshape(8, 16, 128)
        prod = value * state_ref[k].reshape(128, 128)
        total = prod if total is None else total + prod
    part_ref[...] = -total


def sum_kernel(recv_ref, out_ref):
    total = recv_ref[0:8, :]
    for i in range(1, 16):
        total = total + recv_ref[8 * i : 8 * i + 8, :]
    total = total + pltpu.roll(total, 4, 0)
    total = total + pltpu.roll(total, 2, 0)
    for i in range(16):
        out_ref[8 * i : 8 * i + 8, :] = total


VM = pl.BlockSpec(memory_space=pltpu.VMEM)
SM = pl.BlockSpec(memory_space=pltpu.SMEM)
INTERPRET = False


def near(value):
    return pltpu.with_memory_space_constraint(value, pltpu.VMEM)


def call(kernel, outs, in_specs, scratch=(), name=None):
    shapes = [jax.ShapeDtypeStruct(s[1:], F32) if s[0] is None else pltpu.VMEM(s, F32) for s in outs]
    single = len(shapes) == 1
    return pl.pallas_call(
        kernel,
        out_shape=shapes[0] if single else shapes,
        in_specs=in_specs,
        out_specs=VM if single else [VM] * len(shapes),
        scratch_shapes=list(scratch),
        name=name,
        interpret=INTERPRET,
    )


def shards(sources, forward_states, terminal, damping, contact_stiff, regions):
    def over_space(v):
        return lax.all_to_all(v, ("sx", "sy"), 0, 0, tiled=True)

    def over_tm(v):
        slots = v.reshape(NZ * NX4, -1, 128)
        return lax.all_to_all(slots, "tm", 0, 0, tiled=True).reshape(v.shape)

    def scratch(rows):
        return pltpu.VMEM((rows, 128), F32)

    send1 = call(pack_kernel, [(ND, ROWS1, 128)], [SM, SM, VM, VM, VM], [scratch(152)], "pack")(
        contact_stiff, regions, sources, damping, terminal
    )
    recv1 = near(over_space(send1))
    send2, inv1, rhs, fac = call(
        first_kernel,
        [(256, 128), (22, 8, 128), (16, 8, 128), (16, 8, 128)],
        [VM],
        [scratch(320), scratch(320), scratch(256), scratch(192)],
        "first",
    )(recv1)
    inv1, rhs, fac = near(inv1), near(rhs), near(fac)
    recv2 = near(over_tm(send2))
    send3 = call(scan_kernel, [(256, 128)], [VM, VM], name="scan")(recv1, recv2)
    recv3 = near(over_tm(send3))
    send4 = call(final_kernel, [(ND, 32, 128)], [VM] * 5, [scratch(192)], "final")(
        recv1, inv1, rhs, fac, recv3
    )
    recv4 = near(over_space(send4))
    adjoint, part = call(unpack_kernel, [(None, 2, 8, 16, 128), (128, 128)], [VM, VM], name="unpack")(
        recv4, forward_states
    )
    part = near(over_tm(part))
    part = call(sum_kernel, [(128, 128)], [VM], name="sum")(part)
    grad = over_tm(part)
    return adjoint, grad.reshape(8, 16, 128)


def solution(mesh):
    in_specs = (
        P("tm", "sx", "sy", None),
        P("tm", "sx", "sy", None),
        P("sx", "sy", None),
        P("sx", "sy", None),
        P(),
        P("tm", "sx", "sy"),
    )
    out_specs = (P("tm", "sx", "sy", None), P("sx", "sy", None))
    return jax.shard_map(shards, mesh=mesh, in_specs=in_specs, out_specs=out_specs, check_vma=False)
```

time: 151 us -> 126 us (0.83)
  the two profiles are of different devices: /device:TPU:32 before, /device:TPU:2 now
where the time goes in v2:
time: 126 us; the launch traced here: 125 us
  blocking collectives  118 us (94%)
  Pallas kernels  5.87 us (5%)
    all_to_all x4, blocking collectives, over_tm(): return lax.all_to_all(slots, 'tm', 0, 0, tiled=True).reshape(v.shape)  94.3 us
    all_to_all x2, blocking collectives, over_space(): return lax.all_to_all(v, ('sx', 'sy'), 0, 0, tiled=True)  23.9 us

profile of v2, /device:TPU:2, one launch (start us, length us, event | category | flops | bytes accessed | tf_op | source)
XLA Modules:
  0.0 125.3 jit_solution(6445692091072277472)
XLA Ops:
  0.6 1.1 pack.1
  1.8 15.4 %all_to_all.30.recv_ref.recv1_ref = f32[8,144,128]{2,1,0:T(8,128)S(1)} all-to-all(f32[8,144,128]{2,1,0:T(8,128)S(1)} %pack.1), channel_id=1, replica_groups=mesh['tm'=64,'sx'=4,'sy'=2] {'sx','sy'}, dimensions={0} | all-to-all | bytes 1179648 | tf_op jit(solution)/shard_map/all_to_all | solution.py:199
  17.1 2.2 %first.1 = (f32[256,128]{1,0:T(8,128)S(1)}, f32[22,8,128]{2,1,0:T(8,128)S(1)}, f32[16,8,128]{2,1,0:T(8,128)S(1)}, f32[16,8,128]{2,1,0:T(8,128)S(1)}) custom-call(f32[8,144,128]{2,1,0:T(8,128)S(1)} %all_to_all.30.recv_ref.recv1_ref), custom_call_target="tpu_custom_call" | custom-call | tf_op jit(solution)/shard_map/first/pallas_call | solution.py:212
  19.3 35.0 %all_to_all.31 = f32[64,4,128]{2,1,0:T(4,128)S(1)} all-to-all(f32[64,4,128]{2,1,0:T(4,128)S(1)} %bitcast.13), channel_id=1, replica_groups=mesh['tm'=64,'sx'=4,'sy'=2] {'tm'}, dimensions={0} | all-to-all | bytes 262144 | tf_op jit(solution)/shard_map/all_to_all | solution.py:203
  54.3 0.1 scan.1
  54.4 21.1 %all_to_all.32 = f32[64,4,128]{2,1,0:T(4,128)S(1)} all-to-all(f32[64,4,128]{2,1,0:T(4,128)S(1)} %bitcast.9), channel_id=1, replica_groups=mesh['tm'=64,'sx'=4,'sy'=2] {'tm'}, dimensions={0} | all-to-all | bytes 262144 | tf_op jit(solution)/shard_map/all_to_all | solution.py:203
  75.5 0.8 final.1
  76.2 8.5 %all_to_all.33.recv_ref = f32[8,32,128]{2,1,0:T(8,128)S(1)} all-to-all(f32[8,32,128]{2,1,0:T(8,128)S(1)} %final.1), channel_id=1, replica_groups=mesh['tm'=64,'sx'=4,'sy'=2] {'sx','sy'}, dimensions={0} | all-to-all | bytes 262144 | tf_op jit(solution)/shard_map/all_to_all | solution.py:199
  84.8 1.7 %unpack.1 = (f32[2,8,16,128]{3,2,1,0:T(8,128)}, f32[128,128]{1,0:T(8,128)S(1)}) custom-call(f32[8,32,128]{2,1,0:T(8,128)S(1)} %all_to_all.33.recv_ref, f32[2,8,16,128]{3,2,1,0:T(8,128)} %state_ref.1), custom_call_target="tpu_custom_call" | custom-call | tf_op jit(solution)/shard_map/unpack/pallas_call | solution.py:227
  86.4 19.2 %all_to_all.34 = f32[64,2,128]{2,1,0:T(2,128)S(1)} all-to-all(f32[64,2,128]{2,1,0:T(2,128)S(1)} %bitcast.14), channel_id=1, replica_groups=mesh['tm'=64,'sx'=4,'sy'=2] {'tm'}, dimensions={0} | all-to-all | bytes 131072 | tf_op jit(solution)/shard_map/all_to_all | solution.py:203
  105.7 19.0 %all_to_all.35 = f32[64,2,128]{2,1,0:T(2,128)S(1)} all-to-all(f32[64,2,128]{2,1,0:T(2,128)S(1)} %bitcast.12), channel_id=1, replica_groups=mesh['tm'=64,'sx'=4,'sy'=2] {'tm'}, dimensions={0} | all-to-all | bytes 131072 | tf_op jit(solution)/shard_map/all_to_all | solution.py:203
  124.7 0.6 copy.9
  (1 shorter events, 0.0 us)

commit v3 on v2

--- a/solution.py
+++ b/solution.py
@@ -3,6 +3,7 @@
 from jax import lax
 from jax.experimental import pallas as pl
 from jax.experimental.pallas import tpu as pltpu
+from jax.sharding import Mesh
 from jax.sharding import PartitionSpec as P
 
 F32 = jnp.float32
@@ -16,8 +17,10 @@
 DAMP = (32, 40, 12)
 TERM = (72, 40, 12)
 SRC0 = (112, 24, 4)
-REACT = 136
-ROWS1 = 144
+ST0 = (136, 16, 0)
+ST1 = (152, 16, 0)
+REACT = 168
+ROWS1 = 176
 
 
 def xy_neighbours(f):
@@ -56,12 +59,21 @@
     return (t >= 0) & (t < 128)
 
 
-def pack_kernel(stiff_ref, reg_ref, src_ref, damp_ref, term_ref, out_ref, pad):
+def slab():
+    return lax.axis_index("tz") * NX4 + lax.axis_index("tx")
+
+
+def space():
+    return lax.axis_index("sx") * 2 + lax.axis_index("sy")
+
+
+def pack_kernel(stiff_ref, reg_ref, src_ref, damp_ref, term_ref, state_ref, out_ref, pad):
     def put(value, spec):
         off, rows, halo = spec
         pad[halo : halo + 128, :] = value.reshape(128, 128).T
-        pad[halo + 128 : 2 * halo + 128, :] = jnp.zeros((halo, 128), F32)
-        pad[0:halo, :] = jnp.zeros((halo, 128), F32)
+        if halo:
+            pad[halo + 128 : 2 * halo + 128, :] = jnp.zeros((halo, 128), F32)
+            pad[0:halo, :] = jnp.zeros((halo, 128), F32)
         for d in range(ND):
             out_ref[d, off : off + rows, :] = pad[T_OWN * d : T_OWN * d + rows, :]
 
@@ -69,6 +81,8 @@
     put(damp_ref[...], DAMP)
     put(term_ref[...], TERM)
     put(src_ref[0], SRC0)
+    put(state_ref[0], ST0)
+    put(state_ref[1], ST1)
     yl = lax.broadcasted_iota(jnp.int32, (8, 128), 1) % 16
     row = lax.broadcasted_iota(jnp.int32, (8, 128), 0)
     react = []
@@ -86,8 +100,8 @@
 
 
 def first_kernel(recv_ref, out_ref, inv_ref, rhs_ref, fac_ref, scr_d, scr_t, scr1, scr0):
-    d = lax.axis_index("sx") * 2 + lax.axis_index("sy")
-    last = lax.axis_index("tm") == NZ * NX4 - 1
+    d = space()
+    last = slab() == NZ * NX4 - 1
     react1 = recv_ref[:, REACT, :]
     react0 = recv_ref[:, REACT + 1, :]
     damp = spread(scr_d, recv_ref, DAMP[0], DAMP[1])
@@ -112,7 +126,7 @@
 
 
 def scan_kernel(recv1_ref, recv_ref, out_ref):
-    t = lax.axis_index("tm")
+    t = slab()
     s, g = t // 8, t % 8
     sub = lax.broadcasted_iota(jnp.int32, (8, 128), 0)
     low = sub < 4
@@ -132,43 +146,51 @@
         carry = (fac * fac_hi) * carry + (fac * rhs_hi + tile)
 
 
-def final_kernel(recv1_ref, inv_ref, rhs_ref, fac_ref, recv_ref, out_ref, scr):
-    last = lax.axis_index("tm") == NZ * NX4 - 1
+def final_kernel(recv1_ref, inv_ref, rhs_ref, fac_ref, recv_ref, adj_ref, part_ref, scr, scr_o):
+    last = slab() == NZ * NX4 - 1
     for s in range(ND):
         for i in range(3):
             scr[pl.ds(64 * i + s, 8, stride=8), :] = recv_ref[pl.ds(32 * s + i, 8, stride=4), :]
     incoming = scr[...].reshape(24, 8, 128)
     own = fac_ref[...] * incoming[4:20] + rhs_ref[...]
-    scr[0:128, :] = own.reshape(128, 128)
-    for s in range(ND):
-        out_ref[s, 0:16, :] = scr[pl.ds(s, 16, stride=8), :]
+    scr_o[...] = own.reshape(128, 128)
     for s in range(ND):
         scr[pl.ds(s, 24, stride=8), :] = recv1_ref[s, TERM[0] + 8 : TERM[0] + 32, :]
     w = phi(jnp.where(last, scr[...].reshape(24, 8, 128), incoming), inv_ref[...])
     scr[0:128, :] = w.reshape(128, 128)
     for s in range(ND):
-        out_ref[s, 16:32, :] = scr[pl.ds(s, 16, stride=8), :] + recv1_ref[s, SRC1[0] + 8 : SRC1[0] + 24, :]
-
-
-def unpack_kernel(recv_ref, state_ref, adj_ref, part_ref):
-    total = None
+        adj0 = scr_o[pl.ds(s, 16, stride=8), :]
+        adj1 = scr[pl.ds(s, 16, stride=8), :] + recv1_ref[s, SRC1[0] + 8 : SRC1[0] + 24, :]
+        adj_ref[s, 0:16, :] = adj0
+        adj_ref[s, 16:32, :] = adj1
+        part = -(adj0 * recv1_ref[s, ST0[0] : ST0[0] + 16, :] + adj1 * recv1_ref[s, ST1[0] : ST1[0] + 16, :])
+        for x in range(NX4):
+            row = (x * ND + s) * 4
+            part_ref[row : row + 4, :] = part[4 * x : 4 * x + 4]
+
+
+def unpack_kernel(recv_ref, adj_ref, buf, sem):
+    copy = pltpu.make_async_copy(recv_ref.at[:, space()], buf, sem)
+    copy.start()
+    copy.wait()
     for k in range(2):
-        rows = jnp.concatenate([recv_ref[s, 16 * k : 16 * k + 16, :] for s in range(ND)], axis=0)
-        value = rows.T
-        adj_ref[k] = value.reshape(8, 16, 128)
-        prod = value * state_ref[k].reshape(128, 128)
-        total = prod if total is None else total + prod
-    part_ref[...] = -total
+        rows = jnp.concatenate([buf[s, 16 * k : 16 * k + 16, :] for s in range(ND)], axis=0)
+        adj_ref[k] = rows.T.reshape(8, 16, 128)
 
 
 def sum_kernel(recv_ref, out_ref):
-    total = recv_ref[0:8, :]
-    for i in range(1, 16):
-        total = total + recv_ref[8 * i : 8 * i + 8, :]
-    total = total + pltpu.roll(total, 4, 0)
-    total = total + pltpu.roll(total, 2, 0)
-    for i in range(16):
-        out_ref[8 * i : 8 * i + 8, :] = total
+    total = recv_ref[0:32, :]
+    for i in range(1, recv_ref.shape[0] // 32):
+        total = total + recv_ref[32 * i : 32 * i + 32, :]
+    for i in range(out_ref.shape[0] // 32):
+        out_ref[32 * i : 32 * i + 32, :] = total
+
+
+def grad_kernel(recv_ref, out_ref, scr):
+    for x in range(NX4):
+        for d in range(ND):
+            scr[16 * d + 4 * x : 16 * d + 4 * x + 4, :] = recv_ref[32 * x + 4 * d : 32 * x + 4 * d + 4, :]
+    out_ref[...] = scr[...].T.reshape(8, 16, 128)
 
 
 VM = pl.BlockSpec(memory_space=pltpu.VMEM)
@@ -195,20 +217,22 @@
 
 
 def shards(sources, forward_states, terminal, damping, contact_stiff, regions):
-    def over_space(v):
-        return lax.all_to_all(v, ("sx", "sy"), 0, 0, tiled=True)
-
-    def over_tm(v):
-        slots = v.reshape(NZ * NX4, -1, 128)
-        return lax.all_to_all(slots, "tm", 0, 0, tiled=True).reshape(v.shape)
+    def exchange(v, axes):
+        count = 1
+        for axis in axes:
+            count *= lax.axis_size(axis)
+        slots = v.reshape(count, -1, 128)
+        return near(lax.all_to_all(slots, axes, 0, 0, tiled=True).reshape(v.shape))
+
+    tm, xy, plane = ("tz", "tx"), ("sx", "sy"), ("tx", "sx", "sy")
 
     def scratch(rows):
         return pltpu.VMEM((rows, 128), F32)
 
-    send1 = call(pack_kernel, [(ND, ROWS1, 128)], [SM, SM, VM, VM, VM], [scratch(152)], "pack")(
-        contact_stiff, regions, sources, damping, terminal
+    send1 = call(pack_kernel, [(ND, ROWS1, 128)], [SM, SM, VM, VM, VM, VM], [scratch(152)], "pack")(
+        contact_stiff, regions, sources, damping, terminal, forward_states
     )
-    recv1 = near(over_space(send1))
+    recv1 = exchange(send1, xy)
     send2, inv1, rhs, fac = call(
         first_kernel,
         [(256, 128), (22, 8, 128), (16, 8, 128), (16, 8, 128)],
@@ -217,30 +241,36 @@
         "first",
     )(recv1)
     inv1, rhs, fac = near(inv1), near(rhs), near(fac)
-    recv2 = near(over_tm(send2))
+    recv2 = exchange(send2, tm)
     send3 = call(scan_kernel, [(256, 128)], [VM, VM], name="scan")(recv1, recv2)
-    recv3 = near(over_tm(send3))
-    send4 = call(final_kernel, [(ND, 32, 128)], [VM] * 5, [scratch(192)], "final")(
-        recv1, inv1, rhs, fac, recv3
-    )
-    recv4 = near(over_space(send4))
-    adjoint, part = call(unpack_kernel, [(None, 2, 8, 16, 128), (128, 128)], [VM, VM], name="unpack")(
-        recv4, forward_states
-    )
-    part = near(over_tm(part))
-    part = call(sum_kernel, [(128, 128)], [VM], name="sum")(part)
-    grad = over_tm(part)
-    return adjoint, grad.reshape(8, 16, 128)
+    recv3 = exchange(send3, tm)
+    layers, part = call(
+        final_kernel, [(None, ND, 32, 128), (128, 128)], [VM] * 5, [scratch(192), scratch(128)], "final"
+    )(recv1, inv1, rhs, fac, recv3)
+    layers = lax.all_gather(layers, xy, axis=0, tiled=False)
+    adjoint = call(
+        unpack_kernel,
+        [(None, 2, 8, 16, 128)],
+        [pl.BlockSpec(memory_space=pl.ANY)],
+        [pltpu.VMEM((ND, 32, 128), F32), pltpu.SemaphoreType.DMA],
+        "unpack",
+    )(layers)
+    part = call(sum_kernel, [(512, 128)], [VM], name="sum_x")(exchange(part, plane))
+    part = call(sum_kernel, [(128, 128)], [VM], name="sum_z")(exchange(part, ("tz",)))
+    grad = call(grad_kernel, [(None, 8, 16, 128)], [VM], [scratch(128)], "grad")(exchange(part, ("tx",)))
+    return adjoint, grad
 
 
 def solution(mesh):
+    split = Mesh(mesh.devices.reshape(NZ, NX4, 4, 2), ("tz", "tx", "sx", "sy"))
+    tm = ("tz", "tx")
     in_specs = (
-        P("tm", "sx", "sy", None),
-        P("tm", "sx", "sy", None),
+        P(tm, "sx", "sy", None),
+        P(tm, "sx", "sy", None),
         P("sx", "sy", None),
         P("sx", "sy", None),
         P(),
-        P("tm", "sx", "sy"),
+        P(tm, "sx", "sy"),
     )
-    out_specs = (P("tm", "sx", "sy", None), P("sx", "sy", None))
-    return jax.shard_map(shards, mesh=mesh, in_specs=in_specs, out_specs=out_specs, check_vma=False)
+    out_specs = (P(tm, "sx", "sy", None), P("sx", "sy", None))
+    return jax.shard_map(shards, mesh=split, in_specs=in_specs, out_specs=out_specs, check_vma=False)

time: 126 us -> 136 us (1.079)
  the two profiles are of different devices: /device:TPU:2 before, /device:TPU:32 now
where the time goes in v3:
time: 136 us; the launch traced here: 135 us
  blocking collectives  114 us (84%)
  between operations  14.1 us (10%)
  Pallas kernels  7.41 us (5%)
    all_to_all x6, blocking collectives, exchange(): return near(lax.all_to_all(slots, axes, 0, 0, tiled=True).reshape(v.shape))  114 us
  transfers between devices with their start and end apart: 1, of which 0 were waited for; matrix products, arithmetic and copies ran while one was open for 0% of the time, Pallas kernels for 1%

profile of v3, /device:TPU:32, one launch (start us, length us, event | category | flops | bytes accessed | tf_op | source)
XLA Modules:
  0.0 135.4 jit_solution(11705096700872803753)
XLA Ops:
  7.2 0.0 all-gather.3.cloned.1.call-start
  7.2 1.2 pack.1
  8.5 16.8 %all_to_all.30.recv_ref.recv1_ref = f32[8,176,128]{2,1,0:T(8,128)S(1)} all-to-all(f32[8,176,128]{2,1,0:T(8,128)S(1)} %pack.1), channel_id=1, replica_groups=mesh['tz'=16,'tx'=4,'sx'=4,'sy'=2] {'sx','sy'}, dimensions={0} | all-to-all | bytes 1441792 | tf_op jit(solution)/shard_map/all_to_all | solution.py:225
  25.3 2.2 %first.1 = (f32[256,128]{1,0:T(8,128)S(1)}, f32[22,8,128]{2,1,0:T(8,128)S(1)}, f32[16,8,128]{2,1,0:T(8,128)S(1)}, f32[16,8,128]{2,1,0:T(8,128)S(1)}) custom-call(f32[8,176,128]{2,1,0:T(8,128)S(1)} %all_to_all.30.recv_ref.recv1_ref), custom_call_target="tpu_custom_call" | custom-call | tf_op jit(solution)/shard_map/first/pallas_call | solution.py:236
  27.5 34.5 %all_to_all.31 = f32[64,4,128]{2,1,0:T(4,128)S(1)} all-to-all(f32[64,4,128]{2,1,0:T(4,128)S(1)} %bitcast.19), channel_id=1, replica_groups=mesh['tz'=16,'tx'=4,'sx'=4,'sy'=2] {'tz','tx'}, dimensions={0} | all-to-all | bytes 262144 | tf_op jit(solution)/shard_map/all_to_all | solution.py:225
  62.0 0.1 scan.1
  62.1 20.9 %all_to_all.32 = f32[64,4,128]{2,1,0:T(4,128)S(1)} all-to-all(f32[64,4,128]{2,1,0:T(4,128)S(1)} %bitcast.14), channel_id=1, replica_groups=mesh['tz'=16,'tx'=4,'sx'=4,'sy'=2] {'tz','tx'}, dimensions={0} | all-to-all | bytes 262144 | tf_op jit(solution)/shard_map/all_to_all | solution.py:225
  83.0 1.4 %final.1 = (f32[8,32,128]{2,1,0:T(8,128)}, f32[128,128]{1,0:T(8,128)S(1)}) custom-call(f32[8,176,128]{2,1,0:T(8,128)S(1)} %all_to_all.30.recv_ref.recv1_ref, f32[22,8,128]{2,1,0:T(8,128)S(1)} %get-tuple-element.8.inv_ref, f32[16,8,128]{2,1,0:T(8,128)S(1)} %get-tuple-element.9.rhs_ref, f32[16,8,128]{2,1,0:T(8,128)S(1)} %get-tuple-element.10.fac_ref, ...), custom_call_target="tpu_custom_call" | custom-call | tf_op jit(solution)/shard_map/final/pallas_call | solution.py:247
  84.5 0.0 all-gather.3.cloned.1.call-update
  84.5 11.1 %all_to_all.33 = f32[32,4,128]{2,1,0:T(4,128)S(1)} all-to-all(f32[32,4,128]{2,1,0:T(4,128)S(1)} %bitcast.20), channel_id=1, replica_groups=mesh['tz'=16,'tx'=4,'sx'=4,'sy'=2] {'tx','sx','sy'}, dimensions={0} | all-to-all | bytes 131072 | tf_op jit(solution)/shard_map/all_to_all | solution.py:225
  95.6 22.5 %all_to_all.34 = f32[16,32,128]{2,1,0:T(8,128)S(1)} all-to-all(f32[16,32,128]{2,1,0:T(8,128)S(1)} %bitcast.11), channel_id=1, replica_groups=mesh['tz'=16,'tx'=4,'sx'=4,'sy'=2] {'tz'}, dimensions={0} | all-to-all | bytes 524288 | tf_op jit(solution)/shard_map/all_to_all | solution.py:225
  118.1 8.0 %all_to_all.35 = f32[4,32,128]{2,1,0:T(8,128)S(1)} all-to-all(f32[4,32,128]{2,1,0:T(8,128)S(1)} %bitcast.17), channel_id=1, replica_groups=mesh['tz'=16,'tx'=4,'sx'=4,'sy'=2] {'tx'}, dimensions={0} | all-to-all | bytes 131072 | tf_op jit(solution)/shard_map/all_to_all | solution.py:225
  126.1 0.7 grad.1
  126.9 0.0 all-gather.3.cloned.1.call-done
  126.9 1.7 %unpack.1 = f32[2,8,16,128]{3,2,1,0:T(8,128)} custom-call(f32[8,8,32,128]{3,2,1,0:T(8,128)} %bitcast.21), custom_call_target="tpu_custom_call" | custom-call | tf_op jit(solution)/shard_map/unpack/pallas_call | solution.py:251
  (2 shorter events, 0.0 us)
Async XLA Ops:
  7.2 119.7 %all-gather.3.cloned.1.call-start = ((), (), s32[]{:S(2)}) async-start(), calls=%async_computation.6 | async-start | bytes 1179648 | tf_op jit(solution)/shard_map/all_gather | solution.py:250
Sparse Core Ops, SparseCore 0:
  84.6 20.2 all-gather.2

commit v4 on v2

--- a/solution.py
+++ b/solution.py
@@ -3,13 +3,14 @@
 from jax import lax
 from jax.experimental import pallas as pl
 from jax.experimental.pallas import tpu as pltpu
+from jax.sharding import Mesh
 from jax.sharding import PartitionSpec as P
 
 F32 = jnp.float32
 COUPLING = 0.5
 CENTRE = 1.0 + 6.0 * COUPLING
 
-NZ, NX4, ND = 16, 4, 8
+NH, NL, ND = 8, 8, 8
 
 T_OWN = 16
 SRC1 = (0, 32, 8)
@@ -56,6 +57,10 @@
     return (t >= 0) & (t < 128)
 
 
+def is_last_slab():
+    return (lax.axis_index("th") == NH - 1) & (lax.axis_index("tl") == NL - 1)
+
+
 def pack_kernel(stiff_ref, reg_ref, src_ref, damp_ref, term_ref, out_ref, pad):
     def put(value, spec):
         off, rows, halo = spec
@@ -87,7 +92,7 @@
 
 def first_kernel(recv_ref, out_ref, inv_ref, rhs_ref, fac_ref, scr_d, scr_t, scr1, scr0):
     d = lax.axis_index("sx") * 2 + lax.axis_index("sy")
-    last = lax.axis_index("tm") == NZ * NX4 - 1
+    last = is_last_slab()
     react1 = recv_ref[:, REACT, :]
     react0 = recv_ref[:, REACT + 1, :]
     damp = spread(scr_d, recv_ref, DAMP[0], DAMP[1])
@@ -106,37 +111,46 @@
     rhs_ref[...] = rhs[4:20]
     scr_t[0 : 24 * 8, :] = rhs.reshape(24 * 8, 128)
     for s in range(ND):
-        for i in range(3):
-            out_ref[pl.ds(32 * s + i, 8, stride=4), :] = scr_t[pl.ds(64 * i + s, 8, stride=8), :]
-        out_ref[pl.ds(32 * s + 3, 8, stride=4), :] = jnp.broadcast_to(recv_ref[s, REACT + 1 : REACT + 2, :], (8, 128))
-
-
-def scan_kernel(recv1_ref, recv_ref, out_ref):
-    t = lax.axis_index("tm")
-    s, g = t // 8, t % 8
-    sub = lax.broadcasted_iota(jnp.int32, (8, 128), 0)
-    low = sub < 4
-    damp = jnp.zeros((8, 128), F32)
-    for i in range(3):
-        row = recv1_ref[s, pl.ds(DAMP[0] + 8 + 8 * i + g, 1), :]
-        damp = jnp.where(sub % 4 == i, row, damp)
-    carry = jnp.zeros((8, 128), F32)
-    for m in range(31, -1, -1):
-        tile = recv_ref[8 * m : 8 * m + 8, :]
-        react = jnp.where(low, tile[3:4], tile[7:8])
-        fac = 1.0 / (1.0 + 2.0 * (react + damp))
-        fac_hi = pltpu.roll(fac, 4, 0)
-        rhs_hi = pltpu.roll(tile, 4, 0)
-        next_lo = fac_hi * carry + rhs_hi
-        out_ref[8 * m : 8 * m + 8, :] = jnp.where(low, next_lo, pltpu.roll(carry, 4, 0))
-        carry = (fac * fac_hi) * carry + (fac * rhs_hi + tile)
+        out_ref[32 * s : 32 * s + 24, :] = scr_t[pl.ds(s, 24, stride=8), :]
+        out_ref[32 * s + 24 : 32 * s + 32, :] = jnp.broadcast_to(recv_ref[s, REACT + 1 : REACT + 2, :], (8, 128))
+
+
+def own_damp(recv1_ref):
+    return recv1_ref[lax.axis_index("tl"), DAMP[0] + 8 : DAMP[0] + 32, :]
+
+
+def compose_kernel(recv1_ref, recv_ref, out_ref):
+    damp = own_damp(recv1_ref)
+    carry = recv_ref[32 * (NL - 1) : 32 * (NL - 1) + 24, :]
+    for j in range(NL - 2, -1, -1):
+        react = recv_ref[32 * j + 24 : 32 * j + 25, :]
+        carry = carry / (1.0 + 2.0 * (react + damp)) + recv_ref[32 * j : 32 * j + 24, :]
+    tail = jnp.concatenate([recv_ref[32 * j + 24 : 32 * j + 25, :] for j in range(NL)], axis=0)
+    for h in range(NH):
+        out_ref[32 * h : 32 * h + 24, :] = carry
+        out_ref[32 * h + 24 : 32 * h + 32, :] = tail
+
+
+def scan_kernel(recv1_ref, recv2_ref, recv_ref, out_ref):
+    me = lax.axis_index("th")
+    damp = own_damp(recv1_ref)
+    carry = jnp.zeros((24, 128), F32)
+    for h in range(NH - 1, 0, -1):
+        den = None
+        for j in range(NL):
+            term = 1.0 + 2.0 * (recv_ref[32 * h + 24 + j : 32 * h + 25 + j, :] + damp)
+            den = term if den is None else den * term
+        carry = jnp.where(h > me, carry / den + recv_ref[32 * h : 32 * h + 24, :], carry)
+    for j in range(NL - 1, -1, -1):
+        out_ref[24 * j : 24 * j + 24, :] = carry
+        react = recv2_ref[32 * j + 24 : 32 * j + 25, :]
+        carry = carry / (1.0 + 2.0 * (react + damp)) + recv2_ref[32 * j : 32 * j + 24, :]
 
 
 def final_kernel(recv1_ref, inv_ref, rhs_ref, fac_ref, recv_ref, out_ref, scr):
-    last = lax.axis_index("tm") == NZ * NX4 - 1
-    for s in range(ND):
-        for i in range(3):
-            scr[pl.ds(64 * i + s, 8, stride=8), :] = recv_ref[pl.ds(32 * s + i, 8, stride=4), :]
+    last = is_last_slab()
+    for s in range(ND):
+        scr[pl.ds(s, 24, stride=8), :] = recv_ref[24 * s : 24 * s + 24, :]
     incoming = scr[...].reshape(24, 8, 128)
     own = fac_ref[...] * incoming[4:20] + rhs_ref[...]
     scr[0:128, :] = own.reshape(128, 128)
@@ -162,13 +176,11 @@
 
 
 def sum_kernel(recv_ref, out_ref):
-    total = recv_ref[0:8, :]
-    for i in range(1, 16):
-        total = total + recv_ref[8 * i : 8 * i + 8, :]
-    total = total + pltpu.roll(total, 4, 0)
-    total = total + pltpu.roll(total, 2, 0)
-    for i in range(16):
-        out_ref[8 * i : 8 * i + 8, :] = total
+    total = recv_ref[0:16, :]
+    for i in range(1, 8):
+        total = total + recv_ref[16 * i : 16 * i + 16, :]
+    for i in range(8):
+        out_ref[16 * i : 16 * i + 16, :] = total
 
 
 VM = pl.BlockSpec(memory_space=pltpu.VMEM)
@@ -195,12 +207,9 @@
 
 
 def shards(sources, forward_states, terminal, damping, contact_stiff, regions):
-    def over_space(v):
-        return lax.all_to_all(v, ("sx", "sy"), 0, 0, tiled=True)
-
-    def over_tm(v):
-        slots = v.reshape(NZ * NX4, -1, 128)
-        return lax.all_to_all(slots, "tm", 0, 0, tiled=True).reshape(v.shape)
+    def exchange(v, axes):
+        slots = v.reshape(8, -1, 128)
+        return lax.all_to_all(slots, axes, 0, 0, tiled=True).reshape(v.shape)
 
     def scratch(rows):
         return pltpu.VMEM((rows, 128), F32)
@@ -208,7 +217,7 @@
     send1 = call(pack_kernel, [(ND, ROWS1, 128)], [SM, SM, VM, VM, VM], [scratch(152)], "pack")(
         contact_stiff, regions, sources, damping, terminal
     )
-    recv1 = near(over_space(send1))
+    recv1 = near(exchange(send1, ("sx", "sy")))
     send2, inv1, rhs, fac = call(
         first_kernel,
         [(256, 128), (22, 8, 128), (16, 8, 128), (16, 8, 128)],
@@ -217,30 +226,32 @@
         "first",
     )(recv1)
     inv1, rhs, fac = near(inv1), near(rhs), near(fac)
-    recv2 = near(over_tm(send2))
-    send3 = call(scan_kernel, [(256, 128)], [VM, VM], name="scan")(recv1, recv2)
-    recv3 = near(over_tm(send3))
-    send4 = call(final_kernel, [(ND, 32, 128)], [VM] * 5, [scratch(192)], "final")(
-        recv1, inv1, rhs, fac, recv3
-    )
-    recv4 = near(over_space(send4))
+    recv2 = near(exchange(send2, "tl"))
+    send_h = call(compose_kernel, [(256, 128)], [VM, VM], name="compose")(recv1, recv2)
+    recv_h = near(exchange(send_h, "th"))
+    send3 = call(scan_kernel, [(192, 128)], [VM] * 3, name="scan")(recv1, recv2, recv_h)
+    recv3 = near(exchange(send3, "tl"))
+    send4 = call(final_kernel, [(ND, 32, 128)], [VM] * 5, [scratch(192)], "final")(recv1, inv1, rhs, fac, recv3)
+    recv4 = near(exchange(send4, ("sx", "sy")))
     adjoint, part = call(unpack_kernel, [(None, 2, 8, 16, 128), (128, 128)], [VM, VM], name="unpack")(
-        recv4, forward_states
-    )
-    part = near(over_tm(part))
-    part = call(sum_kernel, [(128, 128)], [VM], name="sum")(part)
-    grad = over_tm(part)
+        recv4, near(forward_states)
+    )
+    for axis in ("tl", "th"):
+        part = call(sum_kernel, [(128, 128)], [VM], name="sum_" + axis)(near(exchange(part, axis)))
+    grad = exchange(part, "tl")
     return adjoint, grad.reshape(8, 16, 128)
 
 
 def solution(mesh):
+    split = Mesh(mesh.devices.reshape(NH, NL, 4, 2), ("th", "tl", "sx", "sy"))
+    tm = ("th", "tl")
     in_specs = (
-        P("tm", "sx", "sy", None),
-        P("tm", "sx", "sy", None),
+        P(tm, "sx", "sy", None),
+        P(tm, "sx", "sy", None),
         P("sx", "sy", None),
         P("sx", "sy", None),
         P(),
-        P("tm", "sx", "sy"),
-    )
-    out_specs = (P("tm", "sx", "sy", None), P("sx", "sy", None))
-    return jax.shard_map(shards, mesh=mesh, in_specs=in_specs, out_specs=out_specs, check_vma=False)
+        P(tm, "sx", "sy"),
+    )
+    out_specs = (P(tm, "sx", "sy", None), P("sx", "sy", None))
+    return jax.shard_map(shards, mesh=split, in_specs=in_specs, out_specs=out_specs, check_vma=False)

time: 126 us -> 113 us (0.90)
  blocking collectives: 118 us -> 106 us
    all_to_all x6 -> x8, blocking collectives: 118 us -> 106 us  [exchange(): return lax.all_to_all(slots, axes, 0, 0, tiled=True).reshape(v.shape)]
where the time goes in v4:
time: 113 us
  blocking collectives  106 us (94%)
  Pallas kernels  5.05 us (4%)
    all_to_all x8, blocking collectives, exchange(): return lax.all_to_all(slots, axes, 0, 0, tiled=True).reshape(v.shape)  106 us

profile of v4, /device:TPU:2, one launch (start us, length us, event | category | flops | bytes accessed | tf_op | source)
XLA Modules:
  0.0 112.8 jit_solution(4120690698450058834)
XLA Ops:
  0.6 1.1 pack.1
  1.8 15.4 %all_to_all.40.recv_ref.recv1_ref = f32[8,144,128]{2,1,0:T(8,128)S(1)} all-to-all(f32[8,144,128]{2,1,0:T(8,128)S(1)} %pack.1), channel_id=1, replica_groups=mesh['th'=8,'tl'=8,'sx'=4,'sy'=2] {'sx','sy'}, dimensions={0} | all-to-all | bytes 1179648 | tf_op jit(solution)/shard_map/all_to_all | solution.py:212
  17.1 2.2 %first.1 = (f32[256,128]{1,0:T(8,128)S(1)}, f32[22,8,128]{2,1,0:T(8,128)S(1)}, f32[16,8,128]{2,1,0:T(8,128)S(1)}, f32[16,8,128]{2,1,0:T(8,128)S(1)}) custom-call(f32[8,144,128]{2,1,0:T(8,128)S(1)} %all_to_all.40.recv_ref.recv1_ref), custom_call_target="tpu_custom_call" | custom-call | tf_op jit(solution)/shard_map/first/pallas_call | solution.py:221
  19.3 11.5 %all_to_all.41 = f32[8,32,128]{2,1,0:T(8,128)S(1)} all-to-all(f32[8,32,128]{2,1,0:T(8,128)S(1)} %bitcast.21), channel_id=1, replica_groups=mesh['th'=8,'tl'=8,'sx'=4,'sy'=2] {'tl'}, dimensions={0} | all-to-all | bytes 262144 | tf_op jit(solution)/shard_map/all_to_all | solution.py:212
  30.8 27.8 %all_to_all.42 = f32[8,32,128]{2,1,0:T(8,128)S(1)} all-to-all(f32[8,32,128]{2,1,0:T(8,128)S(1)} %bitcast.13), channel_id=1, replica_groups=mesh['th'=8,'tl'=8,'sx'=4,'sy'=2] {'th'}, dimensions={0} | all-to-all | bytes 262144 | tf_op jit(solution)/shard_map/all_to_all | solution.py:212
  58.6 0.1 scan.1
  58.8 9.0 %all_to_all.43 = f32[8,24,128]{2,1,0:T(8,128)S(1)} all-to-all(f32[8,24,128]{2,1,0:T(8,128)S(1)} %bitcast.15), channel_id=1, replica_groups=mesh['th'=8,'tl'=8,'sx'=4,'sy'=2] {'tl'}, dimensions={0} | all-to-all | bytes 196608 | tf_op jit(solution)/shard_map/all_to_all | solution.py:212
  67.7 0.8 final.1
  68.5 0.0 copy-start
  68.5 8.7 %all_to_all.44.recv_ref = f32[8,32,128]{2,1,0:T(8,128)S(1)} all-to-all(f32[8,32,128]{2,1,0:T(8,128)S(1)} %final.1), channel_id=1, replica_groups=mesh['th'=8,'tl'=8,'sx'=4,'sy'=2] {'sx','sy'}, dimensions={0} | all-to-all | bytes 262144 | tf_op jit(solution)/shard_map/all_to_all | solution.py:212
  77.2 0.0 copy-done
  77.2 0.8 unpack.1
  78.0 8.8 %all_to_all.45 = f32[8,16,128]{2,1,0:T(8,128)S(1)} all-to-all(f32[8,16,128]{2,1,0:T(8,128)S(1)} %bitcast.22), channel_id=1, replica_groups=mesh['th'=8,'tl'=8,'sx'=4,'sy'=2] {'tl'}, dimensions={0} | all-to-all | bytes 131072 | tf_op jit(solution)/shard_map/all_to_all | solution.py:212
  86.8 16.2 %all_to_all.46 = f32[8,16,128]{2,1,0:T(8,128)S(1)} all-to-all(f32[8,16,128]{2,1,0:T(8,128)S(1)} %bitcast.18), channel_id=1, replica_groups=mesh['th'=8,'tl'=8,'sx'=4,'sy'=2] {'th'}, dimensions={0} | all-to-all | bytes 131072 | tf_op jit(solution)/shard_map/all_to_all | solution.py:212
  103.0 9.1 %all_to_all.47 = f32[8,16,128]{2,1,0:T(8,128)S(1)} all-to-all(f32[8,16,128]{2,1,0:T(8,128)S(1)} %bitcast.20), channel_id=1, replica_groups=mesh['th'=8,'tl'=8,'sx'=4,'sy'=2] {'tl'}, dimensions={0} | all-to-all | bytes 131072 | tf_op jit(solution)/shard_map/all_to_all | solution.py:212
  112.2 0.6 copy.9
  (3 shorter events, 0.1 us)
Async XLA Ops:
  68.5 8.7 %copy-start = (f32[2,8,16,128]{3,2,1,0:T(8,128)S(1)}, f32[2,8,16,128]{3,2,1,0:T(8,128)}, u32[]{:S(2)}) copy-start(f32[2,8,16,128]{3,2,1,0:T(8,128)} %state_ref.1) | copy-start | bytes 393220

commit v5 on v4

--- a/solution.py
+++ b/solution.py
@@ -61,6 +61,10 @@
     return (lax.axis_index("th") == NH - 1) & (lax.axis_index("tl") == NL - 1)
 
 
+def space():
+    return lax.axis_index("sx") * 2 + lax.axis_index("sy")
+
+
 def pack_kernel(stiff_ref, reg_ref, src_ref, damp_ref, term_ref, out_ref, pad):
     def put(value, spec):
         off, rows, halo = spec
@@ -91,22 +95,25 @@
 
 
 def first_kernel(recv_ref, out_ref, inv_ref, rhs_ref, fac_ref, scr_d, scr_t, scr1, scr0):
-    d = lax.axis_index("sx") * 2 + lax.axis_index("sy")
-    last = is_last_slab()
+    d = space()
     react1 = recv_ref[:, REACT, :]
     react0 = recv_ref[:, REACT + 1, :]
     damp = spread(scr_d, recv_ref, DAMP[0], DAMP[1])
     inside = row_mask(40, 12, d)
     zero = jnp.zeros((40, 8, 128), F32)
-    inv1 = jnp.where(inside, 1.0 / (CENTRE + (react1[None] + damp)), zero)
-    inv0 = jnp.where(inside, 1.0 / (CENTRE + (react0[None] + damp)), zero)
-    inv_ref[...] = inv1[9:31]
+    inv1 = jnp.where(inside[9:31], 1.0 / (CENTRE + (react1[None] + damp[9:31])), zero[9:31])
+    inv0 = jnp.where(inside[5:35], 1.0 / (CENTRE + (react0[None] + damp[5:35])), zero[5:35])
+    inv_ref[...] = inv1
     fac_ref[...] = 1.0 / (1.0 + 2.0 * (react0[None] + damp[12:28]))
-    term = spread(scr_t, recv_ref, TERM[0], TERM[1])
-    term = jnp.where(last, term, zero)
-    v = phi(term, inv1[1:39])
-    v = v + spread(scr1, recv_ref, SRC1[0], SRC1[1])
-    rhs = phi(v, inv0[5:35])
+    spread(scr1, recv_ref, SRC1[0], SRC1[1])
+
+    @pl.when(is_last_slab())
+    def _():
+        wide = jnp.where(inside, 1.0 / (CENTRE + (react1[None] + damp)), zero)
+        v = phi(spread(scr_t, recv_ref, TERM[0], TERM[1]), wide[1:39])
+        scr1[...] = scr1[...] + v.reshape(256, 128)
+
+    rhs = phi(scr1[...].reshape(32, 8, 128), inv0)
     rhs = rhs + spread(scr0, recv_ref, SRC0[0], SRC0[1])
     rhs_ref[...] = rhs[4:20]
     scr_t[0 : 24 * 8, :] = rhs.reshape(24 * 8, 128)
@@ -125,22 +132,29 @@
     for j in range(NL - 2, -1, -1):
         react = recv_ref[32 * j + 24 : 32 * j + 25, :]
         carry = carry / (1.0 + 2.0 * (react + damp)) + recv_ref[32 * j : 32 * j + 24, :]
-    tail = jnp.concatenate([recv_ref[32 * j + 24 : 32 * j + 25, :] for j in range(NL)], axis=0)
+    group = lax.broadcasted_iota(jnp.int32, (1, 128), 1) // 16
+    tail = recv_ref[24:25, :]
+    for j in range(1, NL):
+        tail = jnp.where(group == j, recv_ref[32 * j + 24 : 32 * j + 25, :], tail)
     for h in range(NH):
-        out_ref[32 * h : 32 * h + 24, :] = carry
-        out_ref[32 * h + 24 : 32 * h + 32, :] = tail
+        out_ref[25 * h : 25 * h + 24, :] = carry
+        out_ref[25 * h + 24 : 25 * h + 25, :] = tail
 
 
 def scan_kernel(recv1_ref, recv2_ref, recv_ref, out_ref):
     me = lax.axis_index("th")
     damp = own_damp(recv1_ref)
     carry = jnp.zeros((24, 128), F32)
+    own_lanes = lax.broadcasted_iota(jnp.int32, (8, 128), 1) // 16 == lax.broadcasted_iota(jnp.int32, (8, 128), 0)
     for h in range(NH - 1, 0, -1):
+        react = jnp.where(own_lanes, recv_ref[25 * h + 24 : 25 * h + 25, :], jnp.zeros((8, 128), F32))
+        for shift in (16, 32, 64):
+            react = react + pltpu.roll(react, shift, 1)
         den = None
         for j in range(NL):
-            term = 1.0 + 2.0 * (recv_ref[32 * h + 24 + j : 32 * h + 25 + j, :] + damp)
+            term = 1.0 + 2.0 * (react[j : j + 1] + damp)
             den = term if den is None else den * term
-        carry = jnp.where(h > me, carry / den + recv_ref[32 * h : 32 * h + 24, :], carry)
+        carry = jnp.where(h > me, carry / den + recv_ref[25 * h : 25 * h + 24, :], carry)
     for j in range(NL - 1, -1, -1):
         out_ref[24 * j : 24 * j + 24, :] = carry
         react = recv2_ref[32 * j + 24 : 32 * j + 25, :]
@@ -208,7 +222,8 @@
 
 def shards(sources, forward_states, terminal, damping, contact_stiff, regions):
     def exchange(v, axes):
-        slots = v.reshape(8, -1, 128)
+        rows = v.size // 1024
+        slots = v.reshape(8, rows, 128) if rows % 8 == 0 else v.reshape(8, 1, rows * 128)
         return lax.all_to_all(slots, axes, 0, 0, tiled=True).reshape(v.shape)
 
     def scratch(rows):
@@ -227,7 +242,7 @@
     )(recv1)
     inv1, rhs, fac = near(inv1), near(rhs), near(fac)
     recv2 = near(exchange(send2, "tl"))
-    send_h = call(compose_kernel, [(256, 128)], [VM, VM], name="compose")(recv1, recv2)
+    send_h = call(compose_kernel, [(200, 128)], [VM, VM], name="compose")(recv1, recv2)
     recv_h = near(exchange(send_h, "th"))
     send3 = call(scan_kernel, [(192, 128)], [VM] * 3, name="scan")(recv1, recv2, recv_h)
     recv3 = near(exchange(send3, "tl"))

time: 113 us -> 111 us (0.982)
    pallas_call x1, Pallas kernels: 2.19 us -> 1.05 us  [shards(): call(first_kernel, [(256, 128), (22, 8, 128), (16, 8, 128), (16, 8, 128)]...]
where the time goes in v5:
time: 111 us
  blocking collectives  105 us (95%)
  Pallas kernels  4.13 us (4%)
    all_to_all x8, blocking collectives, exchange(): return lax.all_to_all(slots, axes, 0, 0, tiled=True).reshape(v.shape)  105 us

profile of v5, /device:TPU:2, one launch (start us, length us, event | category | flops | bytes accessed | tf_op | source)
XLA Modules:
  0.0 110.8 jit_solution(5480429968593413184)
XLA Ops:
  0.6 1.1 %pack.1 = f32[8,144,128]{2,1,0:T(8,128)S(1)} custom-call(f32[8]{0:T(128)} %stiff_ref.1, s32[2,1,2]{2,1,0:T(1,128)} %reg_ref.1, f32[2,8,16,128]{3,2,1,0:T(8,128)} %src_ref.1, f32[8,16,128]{2,1,0:T(8,128)} %damp_ref.1, f32[8,16,128]{2,1,0:T(8,128)} %term_ref.1), custom_call_target="tpu_custom_call" | custom-call | tf_op jit(solution)/shard_map/pack/pallas_call | solution.py:232
  1.8 15.4 %all_to_all.40.recv_ref.recv1_ref = f32[8,144,128]{2,1,0:T(8,128)S(1)} all-to-all(f32[8,144,128]{2,1,0:T(8,128)S(1)} %pack.1), channel_id=1, replica_groups=mesh['th'=8,'tl'=8,'sx'=4,'sy'=2] {'sx','sy'}, dimensions={0} | all-to-all | bytes 1179648 | tf_op jit(solution)/shard_map/all_to_all | solution.py:227
  17.1 1.1 first.1
  18.2 11.5 %all_to_all.41 = f32[8,32,128]{2,1,0:T(8,128)S(1)} all-to-all(f32[8,32,128]{2,1,0:T(8,128)S(1)} %bitcast.21), channel_id=1, replica_groups=mesh['th'=8,'tl'=8,'sx'=4,'sy'=2] {'tl'}, dimensions={0} | all-to-all | bytes 262144 | tf_op jit(solution)/shard_map/all_to_all | solution.py:227
  29.7 27.3 %all_to_all.42 = f32[8,1,3200]{2,1,0:T(1,128)S(1)} all-to-all(f32[8,1,3200]{2,1,0:T(1,128)S(1)} %bitcast.14), channel_id=1, replica_groups=mesh['th'=8,'tl'=8,'sx'=4,'sy'=2] {'th'}, dimensions={0} | all-to-all | bytes 204800 | tf_op jit(solution)/shard_map/all_to_all | solution.py:227
  57.0 0.3 scan.1
  57.4 9.1 %all_to_all.43 = f32[8,24,128]{2,1,0:T(8,128)S(1)} all-to-all(f32[8,24,128]{2,1,0:T(8,128)S(1)} %bitcast.15), channel_id=1, replica_groups=mesh['th'=8,'tl'=8,'sx'=4,'sy'=2] {'tl'}, dimensions={0} | all-to-all | bytes 196608 | tf_op jit(solution)/shard_map/all_to_all | solution.py:227
  66.5 0.8 final.1
  67.3 0.0 copy-start
  67.3 8.7 %all_to_all.44.recv_ref = f32[8,32,128]{2,1,0:T(8,128)S(1)} all-to-all(f32[8,32,128]{2,1,0:T(8,128)S(1)} %final.1), channel_id=1, replica_groups=mesh['th'=8,'tl'=8,'sx'=4,'sy'=2] {'sx','sy'}, dimensions={0} | all-to-all | bytes 262144 | tf_op jit(solution)/shard_map/all_to_all | solution.py:227
  75.9 0.0 copy-done
  75.9 0.8 unpack.1
  76.7 8.8 %all_to_all.45 = f32[8,16,128]{2,1,0:T(8,128)S(1)} all-to-all(f32[8,16,128]{2,1,0:T(8,128)S(1)} %bitcast.22), channel_id=1, replica_groups=mesh['th'=8,'tl'=8,'sx'=4,'sy'=2] {'tl'}, dimensions={0} | all-to-all | bytes 131072 | tf_op jit(solution)/shard_map/all_to_all | solution.py:227
  85.6 15.8 %all_to_all.46 = f32[8,16,128]{2,1,0:T(8,128)S(1)} all-to-all(f32[8,16,128]{2,1,0:T(8,128)S(1)} %bitcast.18), channel_id=1, replica_groups=mesh['th'=8,'tl'=8,'sx'=4,'sy'=2] {'th'}, dimensions={0} | all-to-all | bytes 131072 | tf_op jit(solution)/shard_map/all_to_all | solution.py:227
  101.4 8.7 %all_to_all.47 = f32[8,16,128]{2,1,0:T(8,128)S(1)} all-to-all(f32[8,16,128]{2,1,0:T(8,128)S(1)} %bitcast.20), channel_id=1, replica_groups=mesh['th'=8,'tl'=8,'sx'=4,'sy'=2] {'tl'}, dimensions={0} | all-to-all | bytes 131072 | tf_op jit(solution)/shard_map/all_to_all | solution.py:227
  110.1 0.6 copy.10
  (3 shorter events, 0.1 us)
Async XLA Ops:
  67.3 8.7 %copy-start = (f32[2,8,16,128]{3,2,1,0:T(8,128)S(1)}, f32[2,8,16,128]{3,2,1,0:T(8,128)}, u32[]{:S(2)}) copy-start(f32[2,8,16,128]{3,2,1,0:T(8,128)} %state_ref.1) | copy-start | bytes 393220

commit v6 on v5

--- a/solution.py
+++ b/solution.py
@@ -65,7 +65,7 @@
     return lax.axis_index("sx") * 2 + lax.axis_index("sy")
 
 
-def pack_kernel(stiff_ref, reg_ref, src_ref, damp_ref, term_ref, out_ref, pad):
+def pack_kernel(stiff_ref, reg_ref, src_ref, damp_ref, term_ref, state_ref, out_ref, st_ref, pad, turn):
     def put(value, spec):
         off, rows, halo = spec
         pad[halo : halo + 128, :] = value.reshape(128, 128).T
@@ -86,6 +86,11 @@
     tail = jnp.where(row == 0, react[1], react[0])
     for d in range(ND):
         out_ref[d, REACT : REACT + 8, :] = tail
+    for k in range(2):
+        turn[...] = state_ref[k].reshape(128, 128).T
+        for q in range(NL):
+            for r in range(2):
+                st_ref[pl.ds(32 * q + 2 * k + r, 8, stride=4), :] = turn[pl.ds(2 * q + r, 8, stride=16), :]
 
 
 def spread(scr, recv_ref, off, rows):
@@ -94,7 +99,7 @@
     return scr[0 : rows * 8, :].reshape(rows, 8, 128)
 
 
-def first_kernel(recv_ref, out_ref, inv_ref, rhs_ref, fac_ref, scr_d, scr_t, scr1, scr0):
+def first_kernel(recv_ref, st_ref, out_ref, inv_ref, rhs_ref, fac_ref, src_ref, scr_d, scr_t, scr1, scr0):
     d = space()
     react1 = recv_ref[:, REACT, :]
     react0 = recv_ref[:, REACT + 1, :]
@@ -105,7 +110,7 @@
     inv0 = jnp.where(inside[5:35], 1.0 / (CENTRE + (react0[None] + damp[5:35])), zero[5:35])
     inv_ref[...] = inv1
     fac_ref[...] = 1.0 / (1.0 + 2.0 * (react0[None] + damp[12:28]))
-    spread(scr1, recv_ref, SRC1[0], SRC1[1])
+    src_ref[...] = spread(scr1, recv_ref, SRC1[0], SRC1[1])[8:24]
 
     @pl.when(is_last_slab())
     def _():
@@ -118,8 +123,9 @@
     rhs_ref[...] = rhs[4:20]
     scr_t[0 : 24 * 8, :] = rhs.reshape(24 * 8, 128)
     for s in range(ND):
-        out_ref[32 * s : 32 * s + 24, :] = scr_t[pl.ds(s, 24, stride=8), :]
-        out_ref[32 * s + 24 : 32 * s + 32, :] = jnp.broadcast_to(recv_ref[s, REACT + 1 : REACT + 2, :], (8, 128))
+        out_ref[64 * s : 64 * s + 24, :] = scr_t[pl.ds(s, 24, stride=8), :]
+        out_ref[64 * s + 24 : 64 * s + 32, :] = jnp.broadcast_to(recv_ref[s, REACT + 1 : REACT + 2, :], (8, 128))
+        out_ref[64 * s + 32 : 64 * s + 64, :] = st_ref[32 * s : 32 * s + 32, :]
 
 
 def own_damp(recv1_ref):
@@ -128,14 +134,14 @@
 
 def compose_kernel(recv1_ref, recv_ref, out_ref):
     damp = own_damp(recv1_ref)
-    carry = recv_ref[32 * (NL - 1) : 32 * (NL - 1) + 24, :]
+    carry = recv_ref[64 * (NL - 1) : 64 * (NL - 1) + 24, :]
     for j in range(NL - 2, -1, -1):
-        react = recv_ref[32 * j + 24 : 32 * j + 25, :]
-        carry = carry / (1.0 + 2.0 * (react + damp)) + recv_ref[32 * j : 32 * j + 24, :]
+        react = recv_ref[64 * j + 24 : 64 * j + 25, :]
+        carry = carry / (1.0 + 2.0 * (react + damp)) + recv_ref[64 * j : 64 * j + 24, :]
     group = lax.broadcasted_iota(jnp.int32, (1, 128), 1) // 16
     tail = recv_ref[24:25, :]
     for j in range(1, NL):
-        tail = jnp.where(group == j, recv_ref[32 * j + 24 : 32 * j + 25, :], tail)
+        tail = jnp.where(group == j, recv_ref[64 * j + 24 : 64 * j + 25, :], tail)
     for h in range(NH):
         out_ref[25 * h : 25 * h + 24, :] = carry
         out_ref[25 * h + 24 : 25 * h + 25, :] = tail
@@ -157,44 +163,59 @@
         carry = jnp.where(h > me, carry / den + recv_ref[25 * h : 25 * h + 24, :], carry)
     for j in range(NL - 1, -1, -1):
         out_ref[24 * j : 24 * j + 24, :] = carry
-        react = recv2_ref[32 * j + 24 : 32 * j + 25, :]
-        carry = carry / (1.0 + 2.0 * (react + damp)) + recv2_ref[32 * j : 32 * j + 24, :]
-
-
-def final_kernel(recv1_ref, inv_ref, rhs_ref, fac_ref, recv_ref, out_ref, scr):
-    last = is_last_slab()
+        react = recv2_ref[64 * j + 24 : 64 * j + 25, :]
+        carry = carry / (1.0 + 2.0 * (react + damp)) + recv2_ref[64 * j : 64 * j + 24, :]
+
+
+def final_kernel(recv1_ref, inv_ref, rhs_ref, fac_ref, src_ref, recv_ref, out_ref, scr, layers):
     for s in range(ND):
         scr[pl.ds(s, 24, stride=8), :] = recv_ref[24 * s : 24 * s + 24, :]
-    incoming = scr[...].reshape(24, 8, 128)
-    own = fac_ref[...] * incoming[4:20] + rhs_ref[...]
-    scr[0:128, :] = own.reshape(128, 128)
+    own = fac_ref[...] * scr[32:160, :].reshape(16, 8, 128) + rhs_ref[...]
+    layers[0] = own.reshape(128, 128)
+
+    @pl.when(is_last_slab())
+    def _():
+        for s in range(ND):
+            scr[pl.ds(s, 24, stride=8), :] = recv1_ref[s, TERM[0] + 8 : TERM[0] + 32, :]
+
+    w = phi(scr[...].reshape(24, 8, 128), inv_ref[...]) + src_ref[...]
+    layers[1] = w.reshape(128, 128)
     for s in range(ND):
-        out_ref[s, 0:16, :] = scr[pl.ds(s, 16, stride=8), :]
-    for s in range(ND):
-        scr[pl.ds(s, 24, stride=8), :] = recv1_ref[s, TERM[0] + 8 : TERM[0] + 32, :]
-    w = phi(jnp.where(last, scr[...].reshape(24, 8, 128), incoming), inv_ref[...])
-    scr[0:128, :] = w.reshape(128, 128)
-    for s in range(ND):
-        out_ref[s, 16:32, :] = scr[pl.ds(s, 16, stride=8), :] + recv1_ref[s, SRC1[0] + 8 : SRC1[0] + 24, :]
-
-
-def unpack_kernel(recv_ref, state_ref, adj_ref, part_ref):
-    total = None
+        for k in range(2):
+            for r in range(2):
+                out_ref[pl.ds(4 * s + 2 * k + r, 8, stride=32), :] = layers[k, pl.ds(8 * r + s, 8, stride=16), :]
+
+
+def product_kernel(recv2_ref, recv_ref, out_ref, scr):
+    total = recv_ref[0:32, :] * recv2_ref[32:64, :]
+    for j in range(1, NL):
+        total = total + recv_ref[32 * j : 32 * j + 32, :] * recv2_ref[64 * j + 32 : 64 * j + 64, :]
+    scr[...] = -total
+    for r in range(2):
+        rows = scr[pl.ds(r, 8, stride=4), :] + scr[pl.ds(2 + r, 8, stride=4), :]
+        for h in range(NH):
+            out_ref[16 * h + 8 * r : 16 * h + 8 * r + 8, :] = rows
+
+
+def join_kernel(layers_ref, recv_ref, out_ref):
+    total = recv_ref[0:16, :]
+    for h in range(1, NH):
+        total = total + recv_ref[16 * h : 16 * h + 16, :]
+    for j in range(NL):
+        out_ref[48 * j : 48 * j + 32, :] = layers_ref[32 * j : 32 * j + 32, :]
+        out_ref[48 * j + 32 : 48 * j + 48, :] = total
+
+
+def unpack_kernel(recv_ref, adj_ref, grad_ref, scr):
+    for q in range(NL):
+        for r in range(2):
+            rows = pl.ds(2 * q + r, 8, stride=16)
+            for k in range(2):
+                scr[k, rows, :] = recv_ref[pl.ds(48 * q + 2 * k + r, 8, stride=4), :]
+            scr[2, rows, :] = recv_ref[48 * q + 32 + 8 * r : 48 * q + 40 + 8 * r, :]
     for k in range(2):
-        rows = jnp.concatenate([recv_ref[s, 16 * k : 16 * k + 16, :] for s in range(ND)], axis=0)
-        value = rows.T
-        adj_ref[k] = value.reshape(8, 16, 128)
-        prod = value * state_ref[k].reshape(128, 128)
-        total = prod if total is None else total + prod
-    part_ref[...] = -total
-
-
-def sum_kernel(recv_ref, out_ref):
-    total = recv_ref[0:16, :]
-    for i in range(1, 8):
-        total = total + recv_ref[16 * i : 16 * i + 16, :]
-    for i in range(8):
-        out_ref[16 * i : 16 * i + 16, :] = total
+        adj_ref[k] = scr[k].T.reshape(8, 16, 128)
+    grad_ref[...] = scr[2].T.reshape(8, 16, 128)
 
 
 VM = pl.BlockSpec(memory_space=pltpu.VMEM)
@@ -221,40 +242,49 @@
 
 
 def shards(sources, forward_states, terminal, damping, contact_stiff, regions):
-    def exchange(v, axes):
-        rows = v.size // 1024
-        slots = v.reshape(8, rows, 128) if rows % 8 == 0 else v.reshape(8, 1, rows * 128)
-        return lax.all_to_all(slots, axes, 0, 0, tiled=True).reshape(v.shape)
+    def exchange(v, axes, slots=8):
+        rows = v.size // (128 * slots)
+        whole = rows % 8 == 0 or rows == 4
+        v3 = v.reshape(slots, rows, 128) if whole else v.reshape(slots, 1, rows * 128)
+        return near(lax.all_to_all(v3, axes, 0, 0, tiled=True).reshape(v.shape))
 
     def scratch(rows):
         return pltpu.VMEM((rows, 128), F32)
 
-    send1 = call(pack_kernel, [(ND, ROWS1, 128)], [SM, SM, VM, VM, VM], [scratch(152)], "pack")(
-        contact_stiff, regions, sources, damping, terminal
-    )
-    recv1 = near(exchange(send1, ("sx", "sy")))
-    send2, inv1, rhs, fac = call(
+    xy, group = ("sx", "sy"), ("tl", "sx", "sy")
+    send1, pieces = call(
+        pack_kernel, [(ND, ROWS1, 128), (256, 128)], [SM, SM] + [VM] * 4, [scratch(152), scratch(128)], "pack"
+    )(contact_stiff, regions, sources, damping, terminal, forward_states)
+    recv1 = exchange(send1, xy)
+    send2, inv1, rhs, fac, src1 = call(
         first_kernel,
-        [(256, 128), (22, 8, 128), (16, 8, 128), (16, 8, 128)],
-        [VM],
+        [(512, 128), (22, 8, 128), (16, 8, 128), (16, 8, 128), (16, 8, 128)],
+        [VM, VM],
         [scratch(320), scratch(320), scratch(256), scratch(192)],
         "first",
-    )(recv1)
-    inv1, rhs, fac = near(inv1), near(rhs), near(fac)
-    recv2 = near(exchange(send2, "tl"))
+    )(recv1, near(pieces))
+    recv2 = exchange(send2, "tl")
     send_h = call(compose_kernel, [(200, 128)], [VM, VM], name="compose")(recv1, recv2)
-    recv_h = near(exchange(send_h, "th"))
+    recv_h = exchange(send_h, "th")
     send3 = call(scan_kernel, [(192, 128)], [VM] * 3, name="scan")(recv1, recv2, recv_h)
-    recv3 = near(exchange(send3, "tl"))
-    send4 = call(final_kernel, [(ND, 32, 128)], [VM] * 5, [scratch(192)], "final")(recv1, inv1, rhs, fac, recv3)
-    recv4 = near(exchange(send4, ("sx", "sy")))
-    adjoint, part = call(unpack_kernel, [(None, 2, 8, 16, 128), (128, 128)], [VM, VM], name="unpack")(
-        recv4, near(forward_states)
+    recv3 = exchange(send3, "tl")
+    layers = call(
+        final_kernel, [(256, 128)], [VM] * 6, [scratch(192), pltpu.VMEM((2, 128, 128), F32)], "final"
+    )(recv1, near(inv1), near(rhs), near(fac), near(src1), recv3)
+    layers = exchange(layers, group, 64)
+    part = call(product_kernel, [(128, 128)], [VM, VM], [scratch(32)], "product")(recv2, layers)
+    part = exchange(part, "th")
+    joined = call(join_kernel, [(384, 128)], [VM, VM], name="join")(layers, part)
+    joined = exchange(joined, "tl")
+    return tuple(
+        call(
+            unpack_kernel,
+            [(None, 2, 8, 16, 128), (None, 8, 16, 128)],
+            [VM],
+            [pltpu.VMEM((3, 128, 128), F32)],
+            "unpack",
+        )(joined)
     )
-    for axis in ("tl", "th"):
-        part = call(sum_kernel, [(128, 128)], [VM], name="sum_" + axis)(near(exchange(part, axis)))
-    grad = exchange(part, "tl")
-    return adjoint, grad.reshape(8, 16, 128)
 
 
 def solution(mesh):

time: 111 us -> 108 us (0.973)
  blocking collectives: 105 us -> 102 us
    all_to_all x8 -> x7, blocking collectives: 105 us -> 102 us  [exchange(): return near(lax.all_to_all(v3, axes, 0, 0, tiled=True).reshape(v.shape))]
where the time goes in v6:
time: 108 us; the launch traced here: 107 us
  blocking collectives  102 us (94%)
  Pallas kernels  4.43 us (4%)
    all_to_all x7, blocking collectives, exchange(): return near(lax.all_to_all(v3, axes, 0, 0, tiled=True).reshape(v.shape))  102 us

profile of v6, /device:TPU:2, one launch (start us, length us, event | category | flops | bytes accessed | tf_op | source)
XLA Modules:
  0.0 107.4 jit_solution(5994115351814708308)
XLA Ops:
  0.6 1.3 %pack.1 = (f32[8,144,128]{2,1,0:T(8,128)S(1)}, f32[256,128]{1,0:T(8,128)S(1)}) custom-call(f32[8]{0:T(128)} %stiff_ref.1, s32[2,1,2]{2,1,0:T(1,128)} %reg_ref.1, f32[2,8,16,128]{3,2,1,0:T(8,128)} %src_ref.1, f32[8,16,128]{2,1,0:T(8,128)} %damp_ref.1, f32[8,16,128]{2,1,0:T(8,128)} %term_ref.1, f32[2,8,16,128]{3,2,1,0:T(8,128)} %state_ref.1), custom_call_target="tpu_custom_call" | custom-call | tf_op jit(solution)/shard_map/pack/pallas_call | solution.py:255
  1.9 15.4 %all_to_all.35.recv_ref.recv1_ref = f32[8,144,128]{2,1,0:T(8,128)S(1)} all-to-all(f32[8,144,128]{2,1,0:T(8,128)S(1)} %get-tuple-element.9), channel_id=1, replica_groups=mesh['th'=8,'tl'=8,'sx'=4,'sy'=2] {'sx','sy'}, dimensions={0} | all-to-all | bytes 1179648 | tf_op jit(solution)/shard_map/all_to_all | solution.py:249
  17.3 1.1 first.1
  18.3 12.0 %all_to_all.36 = f32[8,64,128]{2,1,0:T(8,128)S(1)} all-to-all(f32[8,64,128]{2,1,0:T(8,128)S(1)} %bitcast.25), channel_id=1, replica_groups=mesh['th'=8,'tl'=8,'sx'=4,'sy'=2] {'tl'}, dimensions={0} | all-to-all | bytes 524288 | tf_op jit(solution)/shard_map/all_to_all | solution.py:249
  30.4 27.9 %all_to_all.37 = f32[8,1,3200]{2,1,0:T(1,128)S(1)} all-to-all(f32[8,1,3200]{2,1,0:T(1,128)S(1)} %bitcast.21), channel_id=1, replica_groups=mesh['th'=8,'tl'=8,'sx'=4,'sy'=2] {'th'}, dimensions={0} | all-to-all | bytes 204800 | tf_op jit(solution)/shard_map/all_to_all | solution.py:249
  58.3 0.3 scan.1
  58.6 8.3 %all_to_all.38 = f32[8,24,128]{2,1,0:T(8,128)S(1)} all-to-all(f32[8,24,128]{2,1,0:T(8,128)S(1)} %bitcast.23), channel_id=1, replica_groups=mesh['th'=8,'tl'=8,'sx'=4,'sy'=2] {'tl'}, dimensions={0} | all-to-all | bytes 196608 | tf_op jit(solution)/shard_map/all_to_all | solution.py:249
  66.9 0.8 final.1
  67.8 12.6 %all_to_all.39 = f32[64,4,128]{2,1,0:T(4,128)S(1)} all-to-all(f32[64,4,128]{2,1,0:T(4,128)S(1)} %bitcast.19), channel_id=1, replica_groups=mesh['th'=8,'tl'=8,'sx'=4,'sy'=2] {'tl','sx','sy'}, dimensions={0} | all-to-all | bytes 262144 | tf_op jit(solution)/shard_map/all_to_all | solution.py:249
  80.4 16.7 %all_to_all.40 = f32[8,16,128]{2,1,0:T(8,128)S(1)} all-to-all(f32[8,16,128]{2,1,0:T(8,128)S(1)} %bitcast.24), channel_id=1, replica_groups=mesh['th'=8,'tl'=8,'sx'=4,'sy'=2] {'th'}, dimensions={0} | all-to-all | bytes 131072 | tf_op jit(solution)/shard_map/all_to_all | solution.py:249
  97.1 9.4 %all_to_all.41 = f32[8,48,128]{2,1,0:T(8,128)S(1)} all-to-all(f32[8,48,128]{2,1,0:T(8,128)S(1)} %bitcast.18), channel_id=1, replica_groups=mesh['th'=8,'tl'=8,'sx'=4,'sy'=2] {'tl'}, dimensions={0} | all-to-all | bytes 393216 | tf_op jit(solution)/shard_map/all_to_all | solution.py:249
  106.6 0.8 unpack.1
  (3 shorter events, 0.1 us)

commit v7 on v6

--- a/solution.py
+++ b/solution.py
@@ -14,11 +14,11 @@
 
 T_OWN = 16
 SRC1 = (0, 32, 8)
-DAMP = (32, 40, 12)
-TERM = (72, 40, 12)
-SRC0 = (112, 24, 4)
-REACT = 136
-ROWS1 = 144
+TERM = (32, 40, 12)
+SRC0 = (72, 24, 4)
+DAMP = (96, 38, 11)
+REACT = 134
+ROWS1 = 136
 
 
 def xy_neighbours(f):
@@ -65,32 +65,35 @@
     return lax.axis_index("sx") * 2 + lax.axis_index("sy")
 
 
-def pack_kernel(stiff_ref, reg_ref, src_ref, damp_ref, term_ref, state_ref, out_ref, st_ref, pad, turn):
-    def put(value, spec):
-        off, rows, halo = spec
-        pad[halo : halo + 128, :] = value.reshape(128, 128).T
-        pad[halo + 128 : 2 * halo + 128, :] = jnp.zeros((halo, 128), F32)
-        pad[0:halo, :] = jnp.zeros((halo, 128), F32)
-        for d in range(ND):
-            out_ref[d, off : off + rows, :] = pad[T_OWN * d : T_OWN * d + rows, :]
-
-    put(src_ref[1], SRC1)
-    put(damp_ref[...], DAMP)
-    put(term_ref[...], TERM)
-    put(src_ref[0], SRC0)
-    yl = lax.broadcasted_iota(jnp.int32, (8, 128), 1) % 16
-    row = lax.broadcasted_iota(jnp.int32, (8, 128), 0)
+def pack_kernel(stiff_ref, reg_ref, src_hbm, damp_hbm, term_hbm, state_hbm, out_ref, st_ref, pad, turn, arr, sem):
+    parts = (src_hbm.at[1], damp_hbm, term_hbm, src_hbm.at[0], state_hbm.at[0], state_hbm.at[1])
+    copies = [pltpu.make_async_copy(part, arr.at[i], sem.at[i]) for i, part in enumerate(parts)]
+    for copy in copies:
+        copy.start()
+
+    yl = lax.broadcasted_iota(jnp.int32, (2, 128), 1) % 16
+    row = lax.broadcasted_iota(jnp.int32, (2, 128), 0)
     react = []
     for k in range(2):
         react.append(jnp.where(yl < 8, stiff_ref[reg_ref[k, 0, 0]], stiff_ref[reg_ref[k, 0, 1]]))
     tail = jnp.where(row == 0, react[1], react[0])
     for d in range(ND):
-        out_ref[d, REACT : REACT + 8, :] = tail
+        out_ref[d, REACT : REACT + 2, :] = tail
+
+    for i, (off, rows, halo) in enumerate((SRC1, DAMP, TERM, SRC0)):
+        pad[i, 0:halo, :] = jnp.zeros((halo, 128), F32)
+        pad[i, halo + 128 : 2 * halo + 128, :] = jnp.zeros((halo, 128), F32)
+        copies[i].wait()
+        pad[i, halo : halo + 128, :] = arr[i].reshape(128, 128).T
+        for d in range(ND):
+            out_ref[d, off : off + rows, :] = pad[i, T_OWN * d : T_OWN * d + rows, :]
+
     for k in range(2):
-        turn[...] = state_ref[k].reshape(128, 128).T
+        copies[4 + k].wait()
+        turn[k] = arr[4 + k].reshape(128, 128).T
         for q in range(NL):
             for r in range(2):
-                st_ref[pl.ds(32 * q + 2 * k + r, 8, stride=4), :] = turn[pl.ds(2 * q + r, 8, stride=16), :]
+                st_ref[pl.ds(32 * q + 2 * k + r, 8, stride=4), :] = turn[k, pl.ds(2 * q + r, 8, stride=16), :]
 
 
 def spread(scr, recv_ref, off, rows):
@@ -104,18 +107,18 @@
     react1 = recv_ref[:, REACT, :]
     react0 = recv_ref[:, REACT + 1, :]
     damp = spread(scr_d, recv_ref, DAMP[0], DAMP[1])
-    inside = row_mask(40, 12, d)
-    zero = jnp.zeros((40, 8, 128), F32)
-    inv1 = jnp.where(inside[9:31], 1.0 / (CENTRE + (react1[None] + damp[9:31])), zero[9:31])
-    inv0 = jnp.where(inside[5:35], 1.0 / (CENTRE + (react0[None] + damp[5:35])), zero[5:35])
+    inside = row_mask(38, 11, d)
+    zero = jnp.zeros((38, 8, 128), F32)
+    inv1 = jnp.where(inside[8:30], 1.0 / (CENTRE + (react1[None] + damp[8:30])), zero[8:30])
+    inv0 = jnp.where(inside[4:34], 1.0 / (CENTRE + (react0[None] + damp[4:34])), zero[4:34])
     inv_ref[...] = inv1
-    fac_ref[...] = 1.0 / (1.0 + 2.0 * (react0[None] + damp[12:28]))
+    fac_ref[...] = 1.0 / (1.0 + 2.0 * (react0[None] + damp[11:27]))
     src_ref[...] = spread(scr1, recv_ref, SRC1[0], SRC1[1])[8:24]
 
     @pl.when(is_last_slab())
     def _():
         wide = jnp.where(inside, 1.0 / (CENTRE + (react1[None] + damp)), zero)
-        v = phi(spread(scr_t, recv_ref, TERM[0], TERM[1]), wide[1:39])
+        v = phi(spread(scr_t, recv_ref, TERM[0], TERM[1]), wide)
         scr1[...] = scr1[...] + v.reshape(256, 128)
 
     rhs = phi(scr1[...].reshape(32, 8, 128), inv0)
@@ -129,7 +132,7 @@
 
 
 def own_damp(recv1_ref):
-    return recv1_ref[lax.axis_index("tl"), DAMP[0] + 8 : DAMP[0] + 32, :]
+    return recv1_ref[lax.axis_index("tl"), DAMP[0] + 7 : DAMP[0] + 31, :]
 
 
 def compose_kernel(recv1_ref, recv_ref, out_ref):
@@ -206,20 +209,27 @@
         out_ref[48 * j + 32 : 48 * j + 48, :] = total
 
 
-def unpack_kernel(recv_ref, adj_ref, grad_ref, scr):
-    for q in range(NL):
-        for r in range(2):
-            rows = pl.ds(2 * q + r, 8, stride=16)
-            for k in range(2):
-                scr[k, rows, :] = recv_ref[pl.ds(48 * q + 2 * k + r, 8, stride=4), :]
-            scr[2, rows, :] = recv_ref[48 * q + 32 + 8 * r : 48 * q + 40 + 8 * r, :]
-    for k in range(2):
-        adj_ref[k] = scr[k].T.reshape(8, 16, 128)
-    grad_ref[...] = scr[2].T.reshape(8, 16, 128)
+def unpack_kernel(recv_ref, adj_hbm, grad_hbm, scr, out, sem):
+    dests = (adj_hbm.at[0], adj_hbm.at[1], grad_hbm)
+    copies = []
+    for k, dest in enumerate(dests):
+        for q in range(NL):
+            for r in range(2):
+                rows = pl.ds(2 * q + r, 8, stride=16)
+                if k < 2:
+                    scr[k, rows, :] = recv_ref[pl.ds(48 * q + 2 * k + r, 8, stride=4), :]
+                else:
+                    scr[k, rows, :] = recv_ref[48 * q + 32 + 8 * r : 48 * q + 40 + 8 * r, :]
+        out[k] = scr[k].T.reshape(8, 16, 128)
+        copies.append(pltpu.make_async_copy(out.at[k], dest, sem.at[k]))
+        copies[k].start()
+    for copy in copies:
+        copy.wait()
 
 
 VM = pl.BlockSpec(memory_space=pltpu.VMEM)
 SM = pl.BlockSpec(memory_space=pltpu.SMEM)
+HB = pl.BlockSpec(memory_space=pl.ANY)
 INTERPRET = False
 
 
@@ -230,11 +240,12 @@
 def call(kernel, outs, in_specs, scratch=(), name=None):
     shapes = [jax.ShapeDtypeStruct(s[1:], F32) if s[0] is None else pltpu.VMEM(s, F32) for s in outs]
     single = len(shapes) == 1
+    specs = [HB if s[0] is None else VM for s in outs]
     return pl.pallas_call(
         kernel,
         out_shape=shapes[0] if single else shapes,
         in_specs=in_specs,
-        out_specs=VM if single else [VM] * len(shapes),
+        out_specs=specs[0] if single else specs,
         scratch_shapes=list(scratch),
         name=name,
         interpret=INTERPRET,
@@ -253,7 +264,16 @@
 
     xy, group = ("sx", "sy"), ("tl", "sx", "sy")
     send1, pieces = call(
-        pack_kernel, [(ND, ROWS1, 128), (256, 128)], [SM, SM] + [VM] * 4, [scratch(152), scratch(128)], "pack"
+        pack_kernel,
+        [(ND, ROWS1, 128), (256, 128)],
+        [SM, SM] + [HB] * 4,
+        [
+            pltpu.VMEM((4, 152, 128), F32),
+            pltpu.VMEM((2, 128, 128), F32),
+            pltpu.VMEM((6, 8, 16, 128), F32),
+            pltpu.SemaphoreType.DMA((6,)),
+        ],
+        "pack",
     )(contact_stiff, regions, sources, damping, terminal, forward_states)
     recv1 = exchange(send1, xy)
     send2, inv1, rhs, fac, src1 = call(
@@ -281,7 +301,7 @@
             unpack_kernel,
             [(None, 2, 8, 16, 128), (None, 8, 16, 128)],
             [VM],
-            [pltpu.VMEM((3, 128, 128), F32)],
+            [pltpu.VMEM((3, 128, 128), F32), pltpu.VMEM((3, 8, 16, 128), F32), pltpu.SemaphoreType.DMA((3,))],
             "unpack",
         )(joined)
     )

time: 108 us -> 109 us (level)
  no operation moved by 1% of the time
where the time goes in v7:
time: 109 us; the launch traced here: 108 us
  blocking collectives  102 us (94%)
  Pallas kernels  5.45 us (5%)
    all_to_all x7, blocking collectives, exchange(): return near(lax.all_to_all(v3, axes, 0, 0, tiled=True).reshape(v.shape))  102 us
    pallas_call x1, Pallas kernels, shards(): call(pack_kernel, [(ND, ROWS1, 128), (256, 128)], [SM, SM] + [HB] * 4, [p...  2.28 us

profile of v7, /device:TPU:2, one launch (start us, length us, event | category | flops | bytes accessed | tf_op | source)
XLA Modules:
  0.0 108.2 jit_solution(12905274118673462717)
XLA Ops:
  0.6 2.3 %pack.1 = (f32[8,136,128]{2,1,0:T(8,128)S(1)}, f32[256,128]{1,0:T(8,128)S(1)}) custom-call(f32[8]{0:T(128)} %stiff_ref.1, s32[2,1,2]{2,1,0:T(1,128)} %reg_ref.1, f32[2,8,16,128]{3,2,1,0:T(8,128)} %src_hbm.1, f32[8,16,128]{2,1,0:T(8,128)} %damp_hbm.1, f32[8,16,128]{2,1,0:T(8,128)} %term_hbm.1, f32[2,8,16,128]{3,2,1,0:T(8,128)} %state_hbm.1), custom_call_target="tpu_custom_call" | custom-call | tf_op jit(solution)/shard_map/pack/pallas_call | solution.py:266
  2.9 15.0 %all_to_all.35.recv_ref.recv1_ref = f32[8,136,128]{2,1,0:T(8,128)S(1)} all-to-all(f32[8,136,128]{2,1,0:T(8,128)S(1)} %get-tuple-element.9), channel_id=1, replica_groups=mesh['th'=8,'tl'=8,'sx'=4,'sy'=2] {'sx','sy'}, dimensions={0} | all-to-all | bytes 1114112 | tf_op jit(solution)/shard_map/all_to_all | solution.py:260
  17.9 1.1 first.1
  19.0 12.2 %all_to_all.36 = f32[8,64,128]{2,1,0:T(8,128)S(1)} all-to-all(f32[8,64,128]{2,1,0:T(8,128)S(1)} %bitcast.25), channel_id=1, replica_groups=mesh['th'=8,'tl'=8,'sx'=4,'sy'=2] {'tl'}, dimensions={0} | all-to-all | bytes 524288 | tf_op jit(solution)/shard_map/all_to_all | solution.py:260
  31.3 27.8 %all_to_all.37 = f32[8,1,3200]{2,1,0:T(1,128)S(1)} all-to-all(f32[8,1,3200]{2,1,0:T(1,128)S(1)} %bitcast.20), channel_id=1, replica_groups=mesh['th'=8,'tl'=8,'sx'=4,'sy'=2] {'th'}, dimensions={0} | all-to-all | bytes 204800 | tf_op jit(solution)/shard_map/all_to_all | solution.py:260
  59.0 0.3 scan.1
  59.4 8.6 %all_to_all.38 = f32[8,24,128]{2,1,0:T(8,128)S(1)} all-to-all(f32[8,24,128]{2,1,0:T(8,128)S(1)} %bitcast.23), channel_id=1, replica_groups=mesh['th'=8,'tl'=8,'sx'=4,'sy'=2] {'tl'}, dimensions={0} | all-to-all | bytes 196608 | tf_op jit(solution)/shard_map/all_to_all | solution.py:260
  68.0 0.8 final.1
  68.8 12.6 %all_to_all.39 = f32[64,4,128]{2,1,0:T(4,128)S(1)} all-to-all(f32[64,4,128]{2,1,0:T(4,128)S(1)} %bitcast.19), channel_id=1, replica_groups=mesh['th'=8,'tl'=8,'sx'=4,'sy'=2] {'tl','sx','sy'}, dimensions={0} | all-to-all | bytes 262144 | tf_op jit(solution)/shard_map/all_to_all | solution.py:260
  81.5 16.4 %all_to_all.40 = f32[8,16,128]{2,1,0:T(8,128)S(1)} all-to-all(f32[8,16,128]{2,1,0:T(8,128)S(1)} %bitcast.24), channel_id=1, replica_groups=mesh['th'=8,'tl'=8,'sx'=4,'sy'=2] {'th'}, dimensions={0} | all-to-all | bytes 131072 | tf_op jit(solution)/shard_map/all_to_all | solution.py:260
  97.9 9.4 %all_to_all.41 = f32[8,48,128]{2,1,0:T(8,128)S(1)} all-to-all(f32[8,48,128]{2,1,0:T(8,128)S(1)} %bitcast.18), channel_id=1, replica_groups=mesh['th'=8,'tl'=8,'sx'=4,'sy'=2] {'tl'}, dimensions={0} | all-to-all | bytes 393216 | tf_op jit(solution)/shard_map/all_to_all | solution.py:260
  107.4 0.8 unpack.1
  (3 shorter events, 0.1 us)

commit v8 on v6

--- a/solution.py
+++ b/solution.py
@@ -14,11 +14,11 @@
 
 T_OWN = 16
 SRC1 = (0, 32, 8)
-DAMP = (32, 40, 12)
-TERM = (72, 40, 12)
-SRC0 = (112, 24, 4)
-REACT = 136
-ROWS1 = 144
+TERM = (32, 40, 12)
+SRC0 = (72, 24, 4)
+DAMP = (96, 38, 11)
+REACT = 134
+ROWS1 = 136
 
 
 def xy_neighbours(f):
@@ -78,14 +78,14 @@
     put(damp_ref[...], DAMP)
     put(term_ref[...], TERM)
     put(src_ref[0], SRC0)
-    yl = lax.broadcasted_iota(jnp.int32, (8, 128), 1) % 16
-    row = lax.broadcasted_iota(jnp.int32, (8, 128), 0)
+    yl = lax.broadcasted_iota(jnp.int32, (2, 128), 1) % 16
+    row = lax.broadcasted_iota(jnp.int32, (2, 128), 0)
     react = []
     for k in range(2):
         react.append(jnp.where(yl < 8, stiff_ref[reg_ref[k, 0, 0]], stiff_ref[reg_ref[k, 0, 1]]))
     tail = jnp.where(row == 0, react[1], react[0])
     for d in range(ND):
-        out_ref[d, REACT : REACT + 8, :] = tail
+        out_ref[d, REACT : REACT + 2, :] = tail
     for k in range(2):
         turn[...] = state_ref[k].reshape(128, 128).T
         for q in range(NL):
@@ -104,18 +104,18 @@
     react1 = recv_ref[:, REACT, :]
     react0 = recv_ref[:, REACT + 1, :]
     damp = spread(scr_d, recv_ref, DAMP[0], DAMP[1])
-    inside = row_mask(40, 12, d)
-    zero = jnp.zeros((40, 8, 128), F32)
-    inv1 = jnp.where(inside[9:31], 1.0 / (CENTRE + (react1[None] + damp[9:31])), zero[9:31])
-    inv0 = jnp.where(inside[5:35], 1.0 / (CENTRE + (react0[None] + damp[5:35])), zero[5:35])
+    inside = row_mask(38, 11, d)
+    zero = jnp.zeros((38, 8, 128), F32)
+    inv1 = jnp.where(inside[8:30], 1.0 / (CENTRE + (react1[None] + damp[8:30])), zero[8:30])
+    inv0 = jnp.where(inside[4:34], 1.0 / (CENTRE + (react0[None] + damp[4:34])), zero[4:34])
     inv_ref[...] = inv1
-    fac_ref[...] = 1.0 / (1.0 + 2.0 * (react0[None] + damp[12:28]))
+    fac_ref[...] = 1.0 / (1.0 + 2.0 * (react0[None] + damp[11:27]))
     src_ref[...] = spread(scr1, recv_ref, SRC1[0], SRC1[1])[8:24]
 
     @pl.when(is_last_slab())
     def _():
         wide = jnp.where(inside, 1.0 / (CENTRE + (react1[None] + damp)), zero)
-        v = phi(spread(scr_t, recv_ref, TERM[0], TERM[1]), wide[1:39])
+        v = phi(spread(scr_t, recv_ref, TERM[0], TERM[1]), wide)
         scr1[...] = scr1[...] + v.reshape(256, 128)
 
     rhs = phi(scr1[...].reshape(32, 8, 128), inv0)
@@ -129,7 +129,7 @@
 
 
 def own_damp(recv1_ref):
-    return recv1_ref[lax.axis_index("tl"), DAMP[0] + 8 : DAMP[0] + 32, :]
+    return recv1_ref[lax.axis_index("tl"), DAMP[0] + 7 : DAMP[0] + 31, :]
 
 
 def compose_kernel(recv1_ref, recv_ref, out_ref):

time: 108 us -> 108 us (level)
  no operation moved by 1% of the time
where the time goes in v8:
time: 108 us; the launch traced here: 107 us
  blocking collectives  102 us (94%)
  Pallas kernels  4.43 us (4%)
    all_to_all x7, blocking collectives, exchange(): return near(lax.all_to_all(v3, axes, 0, 0, tiled=True).reshape(v.shape))  102 us

profile of v8, /device:TPU:2, one launch (start us, length us, event | category | flops | bytes accessed | tf_op | source)
XLA Modules:
  0.0 107.2 jit_solution(8692506215623598701)
XLA Ops:
  0.6 1.3 %pack.1 = (f32[8,136,128]{2,1,0:T(8,128)S(1)}, f32[256,128]{1,0:T(8,128)S(1)}) custom-call(f32[8]{0:T(128)} %stiff_ref.1, s32[2,1,2]{2,1,0:T(1,128)} %reg_ref.1, f32[2,8,16,128]{3,2,1,0:T(8,128)} %src_ref.1, f32[8,16,128]{2,1,0:T(8,128)} %damp_ref.1, f32[8,16,128]{2,1,0:T(8,128)} %term_ref.1, f32[2,8,16,128]{3,2,1,0:T(8,128)} %state_ref.1), custom_call_target="tpu_custom_call" | custom-call | tf_op jit(solution)/shard_map/pack/pallas_call | solution.py:255
  1.9 15.0 %all_to_all.35.recv_ref.recv1_ref = f32[8,136,128]{2,1,0:T(8,128)S(1)} all-to-all(f32[8,136,128]{2,1,0:T(8,128)S(1)} %get-tuple-element.9), channel_id=1, replica_groups=mesh['th'=8,'tl'=8,'sx'=4,'sy'=2] {'sx','sy'}, dimensions={0} | all-to-all | bytes 1114112 | tf_op jit(solution)/shard_map/all_to_all | solution.py:249
  16.9 1.1 first.1
  18.0 12.2 %all_to_all.36 = f32[8,64,128]{2,1,0:T(8,128)S(1)} all-to-all(f32[8,64,128]{2,1,0:T(8,128)S(1)} %bitcast.25), channel_id=1, replica_groups=mesh['th'=8,'tl'=8,'sx'=4,'sy'=2] {'tl'}, dimensions={0} | all-to-all | bytes 524288 | tf_op jit(solution)/shard_map/all_to_all | solution.py:249
  30.3 27.8 %all_to_all.37 = f32[8,1,3200]{2,1,0:T(1,128)S(1)} all-to-all(f32[8,1,3200]{2,1,0:T(1,128)S(1)} %bitcast.20), channel_id=1, replica_groups=mesh['th'=8,'tl'=8,'sx'=4,'sy'=2] {'th'}, dimensions={0} | all-to-all | bytes 204800 | tf_op jit(solution)/shard_map/all_to_all | solution.py:249
  58.0 0.3 scan.1
  58.4 8.6 %all_to_all.38 = f32[8,24,128]{2,1,0:T(8,128)S(1)} all-to-all(f32[8,24,128]{2,1,0:T(8,128)S(1)} %bitcast.23), channel_id=1, replica_groups=mesh['th'=8,'tl'=8,'sx'=4,'sy'=2] {'tl'}, dimensions={0} | all-to-all | bytes 196608 | tf_op jit(solution)/shard_map/all_to_all | solution.py:249
  67.0 0.8 final.1
  67.8 12.6 %all_to_all.39 = f32[64,4,128]{2,1,0:T(4,128)S(1)} all-to-all(f32[64,4,128]{2,1,0:T(4,128)S(1)} %bitcast.19), channel_id=1, replica_groups=mesh['th'=8,'tl'=8,'sx'=4,'sy'=2] {'tl','sx','sy'}, dimensions={0} | all-to-all | bytes 262144 | tf_op jit(solution)/shard_map/all_to_all | solution.py:249
  80.5 16.4 %all_to_all.40 = f32[8,16,128]{2,1,0:T(8,128)S(1)} all-to-all(f32[8,16,128]{2,1,0:T(8,128)S(1)} %bitcast.24), channel_id=1, replica_groups=mesh['th'=8,'tl'=8,'sx'=4,'sy'=2] {'th'}, dimensions={0} | all-to-all | bytes 131072 | tf_op jit(solution)/shard_map/all_to_all | solution.py:249
  96.9 9.4 %all_to_all.41 = f32[8,48,128]{2,1,0:T(8,128)S(1)} all-to-all(f32[8,48,128]{2,1,0:T(8,128)S(1)} %bitcast.18), channel_id=1, replica_groups=mesh['th'=8,'tl'=8,'sx'=4,'sy'=2] {'tl'}, dimensions={0} | all-to-all | bytes 393216 | tf_op jit(solution)/shard_map/all_to_all | solution.py:249
  106.4 0.8 unpack.1
  (3 shorter events, 0.1 us)

commit v9 on v8

--- a/solution.py
+++ b/solution.py
@@ -21,40 +21,47 @@
 ROWS1 = 136
 
 
-def xy_neighbours(f):
-    sub = lax.broadcasted_iota(jnp.int32, f.shape, 1)
-    lane = lax.broadcasted_iota(jnp.int32, f.shape, 2)
+def neighbours(field):
+    rows = field[0].shape[0]
+    zero = jnp.zeros_like(field[0])
+    lane = lax.broadcasted_iota(jnp.int32, field[0].shape, 1)
     yl = lane % 16
-    xp = pltpu.roll(f, 112, 2)
-    xm = pltpu.roll(f, 16, 2)
-    xpc = pltpu.roll(xp, 6, 1)
-    xmc = pltpu.roll(xm, 2, 1)
-    zero = jnp.zeros_like(f)
-    total = jnp.where(lane < 112, xp, jnp.where(sub < 6, xpc, zero))
-    total = total + jnp.where(lane >= 16, xm, jnp.where(sub >= 2, xmc, zero))
-    yp = pltpu.roll(f, 127, 2)
-    ym = pltpu.roll(f, 1, 2)
-    even = (sub % 2) == 0
-    ypc = pltpu.roll(pltpu.roll(f, 15, 2), 7, 1)
-    ymc = pltpu.roll(pltpu.roll(f, 113, 2), 1, 1)
-    total = total + jnp.where(yl < 15, yp, jnp.where(even, ypc, zero))
-    total = total + jnp.where(yl > 0, ym, jnp.where(even, zero, ymc))
-    return total
+    after = [pltpu.roll(f, 112, 1) for f in field] + [zero, zero]
+    before = [zero, zero] + [pltpu.roll(f, 16, 1) for f in field]
+    out = []
+    for s, f in enumerate(field):
+        total = pltpu.roll(f, 1, 0) + pltpu.roll(f, rows - 1, 0)
+        total = total + jnp.where(lane < 112, after[s], after[s + 2])
+        total = total + jnp.where(lane >= 16, before[s + 2], before[s])
+        other = pltpu.roll(field[s ^ 1], 15 if s % 2 == 0 else 113, 1)
+        total = total + jnp.where(yl < 15, pltpu.roll(f, 127, 1), other if s % 2 == 0 else zero)
+        total = total + jnp.where(yl > 0, pltpu.roll(f, 1, 1), zero if s % 2 == 0 else other)
+        out.append(total)
+    return out
 
 
 def phi(b, inv):
-    n = b.shape[0]
     x = b
-    for s in range(1, 5):
-        nb = x[2:] + x[:-2] + xy_neighbours(x[1:-1])
-        rows = slice(s, n - s)
-        x = (b[rows] + COUPLING * nb) * inv[s - 1 : n - s - 1]
+    for _ in range(4):
+        x = [(b[s] + COUPLING * n) * inv[s] for s, n in enumerate(neighbours(x))]
     return x
 
 
 def row_mask(rows, halo, d):
-    t = lax.broadcasted_iota(jnp.int32, (rows, 8, 128), 0) + d * T_OWN - halo
+    t = lax.broadcasted_iota(jnp.int32, (rows, 128), 0) + d * T_OWN - halo
     return (t >= 0) & (t < 128)
+
+
+def inverse(recv_ref, step, halo, d):
+    rows = T_OWN + 2 * halo
+    first = DAMP[0] + DAMP[2] - halo
+    inside = row_mask(rows, halo, d)
+    out = []
+    for s in range(ND):
+        react = recv_ref[s, REACT + 1 - step : REACT + 2 - step, :]
+        diag = CENTRE + (react + recv_ref[s, first : first + rows, :])
+        out.append(jnp.where(inside, 1.0 / diag, jnp.zeros_like(diag)))
+    return out
 
 
 def is_last_slab():
@@ -93,38 +100,29 @@
                 st_ref[pl.ds(32 * q + 2 * k + r, 8, stride=4), :] = turn[pl.ds(2 * q + r, 8, stride=16), :]
 
 
-def spread(scr, recv_ref, off, rows):
-    for s in range(ND):
-        scr[pl.ds(s, rows, stride=8), :] = recv_ref[s, off : off + rows, :]
-    return scr[0 : rows * 8, :].reshape(rows, 8, 128)
-
-
-def first_kernel(recv_ref, st_ref, out_ref, inv_ref, rhs_ref, fac_ref, src_ref, scr_d, scr_t, scr1, scr0):
+def first_kernel(recv_ref, st_ref, out_ref, inv_ref, rhs_ref, fac_ref, scr):
     d = space()
-    react1 = recv_ref[:, REACT, :]
-    react0 = recv_ref[:, REACT + 1, :]
-    damp = spread(scr_d, recv_ref, DAMP[0], DAMP[1])
-    inside = row_mask(38, 11, d)
-    zero = jnp.zeros((38, 8, 128), F32)
-    inv1 = jnp.where(inside[8:30], 1.0 / (CENTRE + (react1[None] + damp[8:30])), zero[8:30])
-    inv0 = jnp.where(inside[4:34], 1.0 / (CENTRE + (react0[None] + damp[4:34])), zero[4:34])
-    inv_ref[...] = inv1
-    fac_ref[...] = 1.0 / (1.0 + 2.0 * (react0[None] + damp[11:27]))
-    src_ref[...] = spread(scr1, recv_ref, SRC1[0], SRC1[1])[8:24]
+    for s in range(ND):
+        scr[s] = recv_ref[s, SRC1[0] : SRC1[0] + 32, :]
 
     @pl.when(is_last_slab())
     def _():
-        wide = jnp.where(inside, 1.0 / (CENTRE + (react1[None] + damp)), zero)
-        v = phi(spread(scr_t, recv_ref, TERM[0], TERM[1]), wide)
-        scr1[...] = scr1[...] + v.reshape(256, 128)
-
-    rhs = phi(scr1[...].reshape(32, 8, 128), inv0)
-    rhs = rhs + spread(scr0, recv_ref, SRC0[0], SRC0[1])
-    rhs_ref[...] = rhs[4:20]
-    scr_t[0 : 24 * 8, :] = rhs.reshape(24 * 8, 128)
-    for s in range(ND):
-        out_ref[64 * s : 64 * s + 24, :] = scr_t[pl.ds(s, 24, stride=8), :]
-        out_ref[64 * s + 24 : 64 * s + 32, :] = jnp.broadcast_to(recv_ref[s, REACT + 1 : REACT + 2, :], (8, 128))
+        edge = jnp.zeros((1, 128), F32)
+        inv = [jnp.concatenate([edge, v, edge], axis=0) for v in inverse(recv_ref, 1, 11, d)]
+        v = phi([recv_ref[s, TERM[0] : TERM[0] + 40, :] for s in range(ND)], inv)
+        for s in range(ND):
+            scr[s] = scr[s] + v[s][4:36]
+
+    inv1 = inverse(recv_ref, 1, 4, d)
+    rhs = phi([scr[s] for s in range(ND)], inverse(recv_ref, 0, 8, d))
+    for s in range(ND):
+        react0 = recv_ref[s, REACT + 1 : REACT + 2, :]
+        inv_ref[s] = inv1[s]
+        fac_ref[s] = 1.0 / (1.0 + 2.0 * (react0 + recv_ref[s, DAMP[0] + 11 : DAMP[0] + 27, :]))
+        part = rhs[s][4:28] + recv_ref[s, SRC0[0] : SRC0[0] + 24, :]
+        rhs_ref[s] = part[4:20]
+        out_ref[64 * s : 64 * s + 24, :] = part
+        out_ref[64 * s + 24 : 64 * s + 32, :] = jnp.broadcast_to(react0, (8, 128))
         out_ref[64 * s + 32 : 64 * s + 64, :] = st_ref[32 * s : 32 * s + 32, :]
 
 
@@ -167,23 +165,20 @@
         carry = carry / (1.0 + 2.0 * (react + damp)) + recv2_ref[64 * j : 64 * j + 24, :]
 
 
-def final_kernel(recv1_ref, inv_ref, rhs_ref, fac_ref, src_ref, recv_ref, out_ref, scr, layers):
-    for s in range(ND):
-        scr[pl.ds(s, 24, stride=8), :] = recv_ref[24 * s : 24 * s + 24, :]
-    own = fac_ref[...] * scr[32:160, :].reshape(16, 8, 128) + rhs_ref[...]
-    layers[0] = own.reshape(128, 128)
-
-    @pl.when(is_last_slab())
-    def _():
-        for s in range(ND):
-            scr[pl.ds(s, 24, stride=8), :] = recv1_ref[s, TERM[0] + 8 : TERM[0] + 32, :]
-
-    w = phi(scr[...].reshape(24, 8, 128), inv_ref[...]) + src_ref[...]
-    layers[1] = w.reshape(128, 128)
+def final_kernel(recv1_ref, inv_ref, rhs_ref, fac_ref, recv_ref, out_ref, layers):
+    last = is_last_slab()
+    field = []
+    for s in range(ND):
+        incoming = recv_ref[24 * s : 24 * s + 24, :]
+        layers[0, 16 * s : 16 * s + 16, :] = fac_ref[s] * incoming[4:20] + rhs_ref[s]
+        field.append(jnp.where(last, recv1_ref[s, TERM[0] + 8 : TERM[0] + 32, :], incoming))
+    w = phi(field, [inv_ref[s] for s in range(ND)])
+    for s in range(ND):
+        layers[1, 16 * s : 16 * s + 16, :] = w[s][4:20] + recv1_ref[s, SRC1[0] + 8 : SRC1[0] + 24, :]
     for s in range(ND):
         for k in range(2):
             for r in range(2):
-                out_ref[pl.ds(4 * s + 2 * k + r, 8, stride=32), :] = layers[k, pl.ds(8 * r + s, 8, stride=16), :]
+                out_ref[pl.ds(4 * s + 2 * k + r, 8, stride=32), :] = layers[k, pl.ds(16 * s + r, 8, stride=2), :]
 
 
 def product_kernel(recv2_ref, recv_ref, out_ref, scr):
@@ -256,11 +251,11 @@
         pack_kernel, [(ND, ROWS1, 128), (256, 128)], [SM, SM] + [VM] * 4, [scratch(152), scratch(128)], "pack"
     )(contact_stiff, regions, sources, damping, terminal, forward_states)
     recv1 = exchange(send1, xy)
-    send2, inv1, rhs, fac, src1 = call(
+    send2, inv1, rhs, fac = call(
         first_kernel,
-        [(512, 128), (22, 8, 128), (16, 8, 128), (16, 8, 128), (16, 8, 128)],
+        [(512, 128), (8, 24, 128), (8, 16, 128), (8, 16, 128)],
         [VM, VM],
-        [scratch(320), scratch(320), scratch(256), scratch(192)],
+        [pltpu.VMEM((8, 32, 128), F32)],
         "first",
     )(recv1, near(pieces))
     recv2 = exchange(send2, "tl")
@@ -268,9 +263,9 @@
     recv_h = exchange(send_h, "th")
     send3 = call(scan_kernel, [(192, 128)], [VM] * 3, name="scan")(recv1, recv2, recv_h)
     recv3 = exchange(send3, "tl")
-    layers = call(
-        final_kernel, [(256, 128)], [VM] * 6, [scratch(192), pltpu.VMEM((2, 128, 128), F32)], "final"
-    )(recv1, near(inv1), near(rhs), near(fac), near(src1), recv3)
+    layers = call(final_kernel, [(256, 128)], [VM] * 5, [pltpu.VMEM((2, 128, 128), F32)], "final")(
+        recv1, near(inv1), near(rhs), near(fac), recv3
+    )
     layers = exchange(layers, group, 64)
     part = call(product_kernel, [(128, 128)], [VM, VM], [scratch(32)], "product")(recv2, layers)
     part = exchange(part, "th")

time: 108 us -> 107 us (level)
  no operation moved by 1% of the time
where the time goes in v9:
time: 107 us
  blocking collectives  102 us (95%)
  Pallas kernels  4.2 us (4%)
    all_to_all x7, blocking collectives, exchange(): return near(lax.all_to_all(v3, axes, 0, 0, tiled=True).reshape(v.shape))  102 us

profile of v9, /device:TPU:2, one launch (start us, length us, event | category | flops | bytes accessed | tf_op | source)
XLA Modules:
  0.0 107.0 jit_solution(3119373639280640324)
XLA Ops:
  0.6 1.3 %pack.1 = (f32[8,136,128]{2,1,0:T(8,128)S(1)}, f32[256,128]{1,0:T(8,128)S(1)}) custom-call(f32[8]{0:T(128)} %stiff_ref.1, s32[2,1,2]{2,1,0:T(1,128)} %reg_ref.1, f32[2,8,16,128]{3,2,1,0:T(8,128)} %src_ref.1, f32[8,16,128]{2,1,0:T(8,128)} %damp_ref.1, f32[8,16,128]{2,1,0:T(8,128)} %term_ref.1, f32[2,8,16,128]{3,2,1,0:T(8,128)} %state_ref.1), custom_call_target="tpu_custom_call" | custom-call | tf_op jit(solution)/shard_map/pack/pallas_call | solution.py:250
  1.9 15.0 %all_to_all.35.recv_ref.recv1_ref = f32[8,136,128]{2,1,0:T(8,128)S(1)} all-to-all(f32[8,136,128]{2,1,0:T(8,128)S(1)} %get-tuple-element.8), channel_id=1, replica_groups=mesh['th'=8,'tl'=8,'sx'=4,'sy'=2] {'sx','sy'}, dimensions={0} | all-to-all | bytes 1114112 | tf_op jit(solution)/shard_map/all_to_all | solution.py:244
  16.9 0.9 first.1
  17.8 12.2 %all_to_all.36 = f32[8,64,128]{2,1,0:T(8,128)S(1)} all-to-all(f32[8,64,128]{2,1,0:T(8,128)S(1)} %bitcast.25), channel_id=1, replica_groups=mesh['th'=8,'tl'=8,'sx'=4,'sy'=2] {'tl'}, dimensions={0} | all-to-all | bytes 524288 | tf_op jit(solution)/shard_map/all_to_all | solution.py:244
  30.1 27.8 %all_to_all.37 = f32[8,1,3200]{2,1,0:T(1,128)S(1)} all-to-all(f32[8,1,3200]{2,1,0:T(1,128)S(1)} %bitcast.20), channel_id=1, replica_groups=mesh['th'=8,'tl'=8,'sx'=4,'sy'=2] {'th'}, dimensions={0} | all-to-all | bytes 204800 | tf_op jit(solution)/shard_map/all_to_all | solution.py:244
  57.9 0.3 scan.1
  58.2 8.6 %all_to_all.38 = f32[8,24,128]{2,1,0:T(8,128)S(1)} all-to-all(f32[8,24,128]{2,1,0:T(8,128)S(1)} %bitcast.23), channel_id=1, replica_groups=mesh['th'=8,'tl'=8,'sx'=4,'sy'=2] {'tl'}, dimensions={0} | all-to-all | bytes 196608 | tf_op jit(solution)/shard_map/all_to_all | solution.py:244
  66.8 0.8 final.1
  67.6 12.6 %all_to_all.39 = f32[64,4,128]{2,1,0:T(4,128)S(1)} all-to-all(f32[64,4,128]{2,1,0:T(4,128)S(1)} %bitcast.19), channel_id=1, replica_groups=mesh['th'=8,'tl'=8,'sx'=4,'sy'=2] {'tl','sx','sy'}, dimensions={0} | all-to-all | bytes 262144 | tf_op jit(solution)/shard_map/all_to_all | solution.py:244
  80.2 16.4 %all_to_all.40 = f32[8,16,128]{2,1,0:T(8,128)S(1)} all-to-all(f32[8,16,128]{2,1,0:T(8,128)S(1)} %bitcast.24), channel_id=1, replica_groups=mesh['th'=8,'tl'=8,'sx'=4,'sy'=2] {'th'}, dimensions={0} | all-to-all | bytes 131072 | tf_op jit(solution)/shard_map/all_to_all | solution.py:244
  96.7 9.4 %all_to_all.41 = f32[8,48,128]{2,1,0:T(8,128)S(1)} all-to-all(f32[8,48,128]{2,1,0:T(8,128)S(1)} %bitcast.18), channel_id=1, replica_groups=mesh['th'=8,'tl'=8,'sx'=4,'sy'=2] {'tl'}, dimensions={0} | all-to-all | bytes 393216 | tf_op jit(solution)/shard_map/all_to_all | solution.py:244
  106.1 0.8 unpack.1
  (3 shorter events, 0.1 us)

commit v10 on v9

--- a/solution.py
+++ b/solution.py
@@ -121,9 +121,9 @@
         fac_ref[s] = 1.0 / (1.0 + 2.0 * (react0 + recv_ref[s, DAMP[0] + 11 : DAMP[0] + 27, :]))
         part = rhs[s][4:28] + recv_ref[s, SRC0[0] : SRC0[0] + 24, :]
         rhs_ref[s] = part[4:20]
-        out_ref[64 * s : 64 * s + 24, :] = part
-        out_ref[64 * s + 24 : 64 * s + 32, :] = jnp.broadcast_to(react0, (8, 128))
-        out_ref[64 * s + 32 : 64 * s + 64, :] = st_ref[32 * s : 32 * s + 32, :]
+        out_ref[57 * s : 57 * s + 24, :] = part
+        out_ref[57 * s + 24 : 57 * s + 25, :] = react0
+        out_ref[57 * s + 25 : 57 * s + 57, :] = st_ref[32 * s : 32 * s + 32, :]
 
 
 def own_damp(recv1_ref):
@@ -132,14 +132,14 @@
 
 def compose_kernel(recv1_ref, recv_ref, out_ref):
     damp = own_damp(recv1_ref)
-    carry = recv_ref[64 * (NL - 1) : 64 * (NL - 1) + 24, :]
+    carry = recv_ref[57 * (NL - 1) : 57 * (NL - 1) + 24, :]
     for j in range(NL - 2, -1, -1):
-        react = recv_ref[64 * j + 24 : 64 * j + 25, :]
-        carry = carry / (1.0 + 2.0 * (react + damp)) + recv_ref[64 * j : 64 * j + 24, :]
+        react = recv_ref[57 * j + 24 : 57 * j + 25, :]
+        carry = carry * (1.0 / (1.0 + 2.0 * (react + damp))) + recv_ref[57 * j : 57 * j + 24, :]
     group = lax.broadcasted_iota(jnp.int32, (1, 128), 1) // 16
     tail = recv_ref[24:25, :]
     for j in range(1, NL):
-        tail = jnp.where(group == j, recv_ref[64 * j + 24 : 64 * j + 25, :], tail)
+        tail = jnp.where(group == j, recv_ref[57 * j + 24 : 57 * j + 25, :], tail)
     for h in range(NH):
         out_ref[25 * h : 25 * h + 24, :] = carry
         out_ref[25 * h + 24 : 25 * h + 25, :] = tail
@@ -158,11 +158,11 @@
         for j in range(NL):
             term = 1.0 + 2.0 * (react[j : j + 1] + damp)
             den = term if den is None else den * term
-        carry = jnp.where(h > me, carry / den + recv_ref[25 * h : 25 * h + 24, :], carry)
+        carry = jnp.where(h > me, carry * (1.0 / den) + recv_ref[25 * h : 25 * h + 24, :], carry)
     for j in range(NL - 1, -1, -1):
         out_ref[24 * j : 24 * j + 24, :] = carry
-        react = recv2_ref[64 * j + 24 : 64 * j + 25, :]
-        carry = carry / (1.0 + 2.0 * (react + damp)) + recv2_ref[64 * j : 64 * j + 24, :]
+        react = recv2_ref[57 * j + 24 : 57 * j + 25, :]
+        carry = carry * (1.0 / (1.0 + 2.0 * (react + damp))) + recv2_ref[57 * j : 57 * j + 24, :]
 
 
 def final_kernel(recv1_ref, inv_ref, rhs_ref, fac_ref, recv_ref, out_ref, layers):
@@ -182,9 +182,9 @@
 
 
 def product_kernel(recv2_ref, recv_ref, out_ref, scr):
-    total = recv_ref[0:32, :] * recv2_ref[32:64, :]
+    total = recv_ref[0:32, :] * recv2_ref[25:57, :]
     for j in range(1, NL):
-        total = total + recv_ref[32 * j : 32 * j + 32, :] * recv2_ref[64 * j + 32 : 64 * j + 64, :]
+        total = total + recv_ref[32 * j : 32 * j + 32, :] * recv2_ref[57 * j + 25 : 57 * j + 57, :]
     scr[...] = -total
     for r in range(2):
         rows = scr[pl.ds(r, 8, stride=4), :] + scr[pl.ds(2 + r, 8, stride=4), :]
@@ -253,7 +253,7 @@
     recv1 = exchange(send1, xy)
     send2, inv1, rhs, fac = call(
         first_kernel,
-        [(512, 128), (8, 24, 128), (8, 16, 128), (8, 16, 128)],
+        [(456, 128), (8, 24, 128), (8, 16, 128), (8, 16, 128)],
         [VM, VM],
         [pltpu.VMEM((8, 32, 128), F32)],
         "first",

time: 107 us -> 107 us (level)
  no operation moved by 1% of the time
where the time goes in v10:
time: 107 us
  blocking collectives  102 us (95%)
  Pallas kernels  4.22 us (4%)
    all_to_all x7, blocking collectives, exchange(): return near(lax.all_to_all(v3, axes, 0, 0, tiled=True).reshape(v.shape))  102 us

profile of v10, /device:TPU:2, one launch (start us, length us, event | category | flops | bytes accessed | tf_op | source)
XLA Modules:
  0.0 106.7 jit_solution(11495803950382565029)
XLA Ops:
  0.6 1.3 %pack.1 = (f32[8,136,128]{2,1,0:T(8,128)S(1)}, f32[256,128]{1,0:T(8,128)S(1)}) custom-call(f32[8]{0:T(128)} %stiff_ref.1, s32[2,1,2]{2,1,0:T(1,128)} %reg_ref.1, f32[2,8,16,128]{3,2,1,0:T(8,128)} %src_ref.1, f32[8,16,128]{2,1,0:T(8,128)} %damp_ref.1, f32[8,16,128]{2,1,0:T(8,128)} %term_ref.1, f32[2,8,16,128]{3,2,1,0:T(8,128)} %state_ref.1), custom_call_target="tpu_custom_call" | custom-call | tf_op jit(solution)/shard_map/pack/pallas_call | solution.py:250
  1.9 15.0 %all_to_all.35.recv_ref.recv1_ref = f32[8,136,128]{2,1,0:T(8,128)S(1)} all-to-all(f32[8,136,128]{2,1,0:T(8,128)S(1)} %get-tuple-element.8), channel_id=1, replica_groups=mesh['th'=8,'tl'=8,'sx'=4,'sy'=2] {'sx','sy'}, dimensions={0} | all-to-all | bytes 1114112 | tf_op jit(solution)/shard_map/all_to_all | solution.py:244
  16.9 0.9 first.1
  17.8 12.0 %all_to_all.36 = f32[8,1,7296]{2,1,0:T(1,128)S(1)} all-to-all(f32[8,1,7296]{2,1,0:T(1,128)S(1)} %bitcast.26), channel_id=1, replica_groups=mesh['th'=8,'tl'=8,'sx'=4,'sy'=2] {'tl'}, dimensions={0} | all-to-all | bytes 466944 | tf_op jit(solution)/shard_map/all_to_all | solution.py:244
  29.9 27.8 %all_to_all.37 = f32[8,1,3200]{2,1,0:T(1,128)S(1)} all-to-all(f32[8,1,3200]{2,1,0:T(1,128)S(1)} %bitcast.20), channel_id=1, replica_groups=mesh['th'=8,'tl'=8,'sx'=4,'sy'=2] {'th'}, dimensions={0} | all-to-all | bytes 204800 | tf_op jit(solution)/shard_map/all_to_all | solution.py:244
  57.6 0.3 scan.1
  58.0 8.5 %all_to_all.38 = f32[8,24,128]{2,1,0:T(8,128)S(1)} all-to-all(f32[8,24,128]{2,1,0:T(8,128)S(1)} %bitcast.23), channel_id=1, replica_groups=mesh['th'=8,'tl'=8,'sx'=4,'sy'=2] {'tl'}, dimensions={0} | all-to-all | bytes 196608 | tf_op jit(solution)/shard_map/all_to_all | solution.py:244
  66.4 0.8 final.1
  67.2 12.6 %all_to_all.39 = f32[64,4,128]{2,1,0:T(4,128)S(1)} all-to-all(f32[64,4,128]{2,1,0:T(4,128)S(1)} %bitcast.19), channel_id=1, replica_groups=mesh['th'=8,'tl'=8,'sx'=4,'sy'=2] {'tl','sx','sy'}, dimensions={0} | all-to-all | bytes 262144 | tf_op jit(solution)/shard_map/all_to_all | solution.py:244
  79.9 16.5 %all_to_all.40 = f32[8,16,128]{2,1,0:T(8,128)S(1)} all-to-all(f32[8,16,128]{2,1,0:T(8,128)S(1)} %bitcast.25), channel_id=1, replica_groups=mesh['th'=8,'tl'=8,'sx'=4,'sy'=2] {'th'}, dimensions={0} | all-to-all | bytes 131072 | tf_op jit(solution)/shard_map/all_to_all | solution.py:244
  96.4 9.4 %all_to_all.41 = f32[8,48,128]{2,1,0:T(8,128)S(1)} all-to-all(f32[8,48,128]{2,1,0:T(8,128)S(1)} %bitcast.18), channel_id=1, replica_groups=mesh['th'=8,'tl'=8,'sx'=4,'sy'=2] {'tl'}, dimensions={0} | all-to-all | bytes 393216 | tf_op jit(solution)/shard_map/all_to_all | solution.py:244
  105.8 0.8 unpack.1
  (3 shorter events, 0.1 us)

commit v11 on v9

--- a/solution.py
+++ b/solution.py
@@ -41,9 +41,11 @@
 
 
 def phi(b, inv):
+    fixed = [b[s] * inv[s] for s in range(ND)]
+    scale = [COUPLING * inv[s] for s in range(ND)]
     x = b
     for _ in range(4):
-        x = [(b[s] + COUPLING * n) * inv[s] for s, n in enumerate(neighbours(x))]
+        x = [fixed[s] + scale[s] * n for s, n in enumerate(neighbours(x))]
     return x
 
 

time: 107 us -> 107 us (level)
  no operation moved by 1% of the time
where the time goes in v11:
time: 107 us
  blocking collectives  102 us (95%)
  Pallas kernels  4.2 us (4%)
    all_to_all x7, blocking collectives, exchange(): return near(lax.all_to_all(v3, axes, 0, 0, tiled=True).reshape(v.shape))  102 us

profile of v11, /device:TPU:2, one launch (start us, length us, event | category | flops | bytes accessed | tf_op | source)
XLA Modules:
  0.0 107.0 jit_solution(10482593065937282388)
XLA Ops:
  0.6 1.3 %pack.1 = (f32[8,136,128]{2,1,0:T(8,128)S(1)}, f32[256,128]{1,0:T(8,128)S(1)}) custom-call(f32[8]{0:T(128)} %stiff_ref.1, s32[2,1,2]{2,1,0:T(1,128)} %reg_ref.1, f32[2,8,16,128]{3,2,1,0:T(8,128)} %src_ref.1, f32[8,16,128]{2,1,0:T(8,128)} %damp_ref.1, f32[8,16,128]{2,1,0:T(8,128)} %term_ref.1, f32[2,8,16,128]{3,2,1,0:T(8,128)} %state_ref.1), custom_call_target="tpu_custom_call" | custom-call | tf_op jit(solution)/shard_map/pack/pallas_call | solution.py:252
  1.9 15.0 %all_to_all.35.recv_ref.recv1_ref = f32[8,136,128]{2,1,0:T(8,128)S(1)} all-to-all(f32[8,136,128]{2,1,0:T(8,128)S(1)} %get-tuple-element.8), channel_id=1, replica_groups=mesh['th'=8,'tl'=8,'sx'=4,'sy'=2] {'sx','sy'}, dimensions={0} | all-to-all | bytes 1114112 | tf_op jit(solution)/shard_map/all_to_all | solution.py:246
  16.9 0.9 first.1
  17.8 12.2 %all_to_all.36 = f32[8,64,128]{2,1,0:T(8,128)S(1)} all-to-all(f32[8,64,128]{2,1,0:T(8,128)S(1)} %bitcast.25), channel_id=1, replica_groups=mesh['th'=8,'tl'=8,'sx'=4,'sy'=2] {'tl'}, dimensions={0} | all-to-all | bytes 524288 | tf_op jit(solution)/shard_map/all_to_all | solution.py:246
  30.1 27.8 %all_to_all.37 = f32[8,1,3200]{2,1,0:T(1,128)S(1)} all-to-all(f32[8,1,3200]{2,1,0:T(1,128)S(1)} %bitcast.20), channel_id=1, replica_groups=mesh['th'=8,'tl'=8,'sx'=4,'sy'=2] {'th'}, dimensions={0} | all-to-all | bytes 204800 | tf_op jit(solution)/shard_map/all_to_all | solution.py:246
  57.9 0.3 scan.1
  58.2 8.6 %all_to_all.38 = f32[8,24,128]{2,1,0:T(8,128)S(1)} all-to-all(f32[8,24,128]{2,1,0:T(8,128)S(1)} %bitcast.23), channel_id=1, replica_groups=mesh['th'=8,'tl'=8,'sx'=4,'sy'=2] {'tl'}, dimensions={0} | all-to-all | bytes 196608 | tf_op jit(solution)/shard_map/all_to_all | solution.py:246
  66.8 0.8 final.1
  67.6 12.6 %all_to_all.39 = f32[64,4,128]{2,1,0:T(4,128)S(1)} all-to-all(f32[64,4,128]{2,1,0:T(4,128)S(1)} %bitcast.19), channel_id=1, replica_groups=mesh['th'=8,'tl'=8,'sx'=4,'sy'=2] {'tl','sx','sy'}, dimensions={0} | all-to-all | bytes 262144 | tf_op jit(solution)/shard_map/all_to_all | solution.py:246
  80.2 16.4 %all_to_all.40 = f32[8,16,128]{2,1,0:T(8,128)S(1)} all-to-all(f32[8,16,128]{2,1,0:T(8,128)S(1)} %bitcast.24), channel_id=1, replica_groups=mesh['th'=8,'tl'=8,'sx'=4,'sy'=2] {'th'}, dimensions={0} | all-to-all | bytes 131072 | tf_op jit(solution)/shard_map/all_to_all | solution.py:246
  96.7 9.4 %all_to_all.41 = f32[8,48,128]{2,1,0:T(8,128)S(1)} all-to-all(f32[8,48,128]{2,1,0:T(8,128)S(1)} %bitcast.18), channel_id=1, replica_groups=mesh['th'=8,'tl'=8,'sx'=4,'sy'=2] {'tl'}, dimensions={0} | all-to-all | bytes 393216 | tf_op jit(solution)/shard_map/all_to_all | solution.py:246
  106.1 0.8 unpack.1
  (3 shorter events, 0.1 us)

commit v12 on v9

--- a/solution.py
+++ b/solution.py
@@ -97,7 +97,8 @@
         turn[...] = state_ref[k].reshape(128, 128).T
         for q in range(NL):
             for r in range(2):
-                st_ref[pl.ds(32 * q + 2 * k + r, 8, stride=4), :] = turn[pl.ds(2 * q + r, 8, stride=16), :]
+                row = 128 * k + 16 * q + 8 * r
+                st_ref[row : row + 8, :] = turn[pl.ds(2 * q + r, 8, stride=16), :]
 
 
 def first_kernel(recv_ref, st_ref, out_ref, inv_ref, rhs_ref, fac_ref, scr):
@@ -121,9 +122,9 @@
         fac_ref[s] = 1.0 / (1.0 + 2.0 * (react0 + recv_ref[s, DAMP[0] + 11 : DAMP[0] + 27, :]))
         part = rhs[s][4:28] + recv_ref[s, SRC0[0] : SRC0[0] + 24, :]
         rhs_ref[s] = part[4:20]
-        out_ref[64 * s : 64 * s + 24, :] = part
-        out_ref[64 * s + 24 : 64 * s + 32, :] = jnp.broadcast_to(react0, (8, 128))
-        out_ref[64 * s + 32 : 64 * s + 64, :] = st_ref[32 * s : 32 * s + 32, :]
+        out_ref[41 * s : 41 * s + 24, :] = part
+        out_ref[41 * s + 24 : 41 * s + 25, :] = react0
+        out_ref[41 * s + 25 : 41 * s + 41, :] = st_ref[16 * s : 16 * s + 16, :]
 
 
 def own_damp(recv1_ref):
@@ -132,20 +133,20 @@
 
 def compose_kernel(recv1_ref, recv_ref, out_ref):
     damp = own_damp(recv1_ref)
-    carry = recv_ref[64 * (NL - 1) : 64 * (NL - 1) + 24, :]
+    carry = recv_ref[41 * (NL - 1) : 41 * (NL - 1) + 24, :]
     for j in range(NL - 2, -1, -1):
-        react = recv_ref[64 * j + 24 : 64 * j + 25, :]
-        carry = carry / (1.0 + 2.0 * (react + damp)) + recv_ref[64 * j : 64 * j + 24, :]
+        react = recv_ref[41 * j + 24 : 41 * j + 25, :]
+        carry = carry / (1.0 + 2.0 * (react + damp)) + recv_ref[41 * j : 41 * j + 24, :]
     group = lax.broadcasted_iota(jnp.int32, (1, 128), 1) // 16
     tail = recv_ref[24:25, :]
     for j in range(1, NL):
-        tail = jnp.where(group == j, recv_ref[64 * j + 24 : 64 * j + 25, :], tail)
+        tail = jnp.where(group == j, recv_ref[41 * j + 24 : 41 * j + 25, :], tail)
     for h in range(NH):
         out_ref[25 * h : 25 * h + 24, :] = carry
         out_ref[25 * h + 24 : 25 * h + 25, :] = tail
 
 
-def scan_kernel(recv1_ref, recv2_ref, recv_ref, out_ref):
+def scan_kernel(recv1_ref, recv2_ref, recv_ref, st_ref, out_ref):
     me = lax.axis_index("th")
     damp = own_damp(recv1_ref)
     carry = jnp.zeros((24, 128), F32)
@@ -160,16 +161,17 @@
             den = term if den is None else den * term
         carry = jnp.where(h > me, carry / den + recv_ref[25 * h : 25 * h + 24, :], carry)
     for j in range(NL - 1, -1, -1):
-        out_ref[24 * j : 24 * j + 24, :] = carry
-        react = recv2_ref[64 * j + 24 : 64 * j + 25, :]
-        carry = carry / (1.0 + 2.0 * (react + damp)) + recv2_ref[64 * j : 64 * j + 24, :]
+        out_ref[40 * j : 40 * j + 24, :] = carry
+        out_ref[40 * j + 24 : 40 * j + 40, :] = st_ref[128 + 16 * j : 144 + 16 * j, :]
+        react = recv2_ref[41 * j + 24 : 41 * j + 25, :]
+        carry = carry / (1.0 + 2.0 * (react + damp)) + recv2_ref[41 * j : 41 * j + 24, :]
 
 
 def final_kernel(recv1_ref, inv_ref, rhs_ref, fac_ref, recv_ref, out_ref, layers):
     last = is_last_slab()
     field = []
     for s in range(ND):
-        incoming = recv_ref[24 * s : 24 * s + 24, :]
+        incoming = recv_ref[40 * s : 40 * s + 24, :]
         layers[0, 16 * s : 16 * s + 16, :] = fac_ref[s] * incoming[4:20] + rhs_ref[s]
         field.append(jnp.where(last, recv1_ref[s, TERM[0] + 8 : TERM[0] + 32, :], incoming))
     w = phi(field, [inv_ref[s] for s in range(ND)])
@@ -181,15 +183,15 @@
                 out_ref[pl.ds(4 * s + 2 * k + r, 8, stride=32), :] = layers[k, pl.ds(16 * s + r, 8, stride=2), :]
 
 
-def product_kernel(recv2_ref, recv_ref, out_ref, scr):
-    total = recv_ref[0:32, :] * recv2_ref[32:64, :]
-    for j in range(1, NL):
-        total = total + recv_ref[32 * j : 32 * j + 32, :] * recv2_ref[64 * j + 32 : 64 * j + 64, :]
-    scr[...] = -total
+def product_kernel(recv2_ref, recv3_ref, recv_ref, out_ref):
     for r in range(2):
-        rows = scr[pl.ds(r, 8, stride=4), :] + scr[pl.ds(2 + r, 8, stride=4), :]
+        total = jnp.zeros((8, 128), F32)
+        for j in range(NL):
+            first, second = 41 * j + 25 + 8 * r, 40 * j + 24 + 8 * r
+            total = total + recv_ref[pl.ds(32 * j + r, 8, stride=4), :] * recv2_ref[first : first + 8, :]
+            total = total + recv_ref[pl.ds(32 * j + 2 + r, 8, stride=4), :] * recv3_ref[second : second + 8, :]
         for h in range(NH):
-            out_ref[16 * h + 8 * r : 16 * h + 8 * r + 8, :] = rows
+            out_ref[16 * h + 8 * r : 16 * h + 8 * r + 8, :] = -total
 
 
 def join_kernel(layers_ref, recv_ref, out_ref):
@@ -250,24 +252,25 @@
     send1, pieces = call(
         pack_kernel, [(ND, ROWS1, 128), (256, 128)], [SM, SM] + [VM] * 4, [scratch(152), scratch(128)], "pack"
     )(contact_stiff, regions, sources, damping, terminal, forward_states)
+    pieces = near(pieces)
     recv1 = exchange(send1, xy)
     send2, inv1, rhs, fac = call(
         first_kernel,
-        [(512, 128), (8, 24, 128), (8, 16, 128), (8, 16, 128)],
+        [(328, 128), (8, 24, 128), (8, 16, 128), (8, 16, 128)],
         [VM, VM],
         [pltpu.VMEM((8, 32, 128), F32)],
         "first",
-    )(recv1, near(pieces))
+    )(recv1, pieces)
     recv2 = exchange(send2, "tl")
     send_h = call(compose_kernel, [(200, 128)], [VM, VM], name="compose")(recv1, recv2)
     recv_h = exchange(send_h, "th")
-    send3 = call(scan_kernel, [(192, 128)], [VM] * 3, name="scan")(recv1, recv2, recv_h)
+    send3 = call(scan_kernel, [(320, 128)], [VM] * 4, name="scan")(recv1, recv2, recv_h, pieces)
     recv3 = exchange(send3, "tl")
     layers = call(final_kernel, [(256, 128)], [VM] * 5, [pltpu.VMEM((2, 128, 128), F32)], "final")(
         recv1, near(inv1), near(rhs), near(fac), recv3
     )
     layers = exchange(layers, group, 64)
-    part = call(product_kernel, [(128, 128)], [VM, VM], [scratch(32)], "product")(recv2, layers)
+    part = call(product_kernel, [(128, 128)], [VM] * 3, name="product")(recv2, recv3, layers)
     part = exchange(part, "th")
     joined = call(join_kernel, [(384, 128)], [VM, VM], name="join")(layers, part)
     joined = exchange(joined, "tl")

time: 107 us -> 107 us (level)
  no operation moved by 1% of the time
where the time goes in v12:
time: 107 us
  blocking collectives  102 us (95%)
  Pallas kernels  4.22 us (4%)
    all_to_all x7, blocking collectives, exchange(): return near(lax.all_to_all(v3, axes, 0, 0, tiled=True).reshape(v.shape))  102 us

profile of v12, /device:TPU:2, one launch (start us, length us, event | category | flops | bytes accessed | tf_op | source)
XLA Modules:
  0.0 106.7 jit_solution(6430040292969513918)
XLA Ops:
  0.6 1.3 %pack.1 = (f32[8,136,128]{2,1,0:T(8,128)S(1)}, f32[256,128]{1,0:T(8,128)S(1)}) custom-call(f32[8]{0:T(128)} %stiff_ref.1, s32[2,1,2]{2,1,0:T(1,128)} %reg_ref.1, f32[2,8,16,128]{3,2,1,0:T(8,128)} %src_ref.1, f32[8,16,128]{2,1,0:T(8,128)} %damp_ref.1, f32[8,16,128]{2,1,0:T(8,128)} %term_ref.1, f32[2,8,16,128]{3,2,1,0:T(8,128)} %state_ref.1), custom_call_target="tpu_custom_call" | custom-call | tf_op jit(solution)/shard_map/pack/pallas_call | solution.py:252
  1.9 15.0 %all_to_all.35.recv_ref.recv1_ref = f32[8,136,128]{2,1,0:T(8,128)S(1)} all-to-all(f32[8,136,128]{2,1,0:T(8,128)S(1)} %get-tuple-element.8), channel_id=1, replica_groups=mesh['th'=8,'tl'=8,'sx'=4,'sy'=2] {'sx','sy'}, dimensions={0} | all-to-all | bytes 1114112 | tf_op jit(solution)/shard_map/all_to_all | solution.py:246
  16.9 0.9 first.1
  17.8 11.6 %all_to_all.36 = f32[8,1,5248]{2,1,0:T(1,128)S(1)} all-to-all(f32[8,1,5248]{2,1,0:T(1,128)S(1)} %bitcast.27), channel_id=1, replica_groups=mesh['th'=8,'tl'=8,'sx'=4,'sy'=2] {'tl'}, dimensions={0} | all-to-all | bytes 335872 | tf_op jit(solution)/shard_map/all_to_all | solution.py:246
  29.4 27.9 %all_to_all.37 = f32[8,1,3200]{2,1,0:T(1,128)S(1)} all-to-all(f32[8,1,3200]{2,1,0:T(1,128)S(1)} %bitcast.24), channel_id=1, replica_groups=mesh['th'=8,'tl'=8,'sx'=4,'sy'=2] {'th'}, dimensions={0} | all-to-all | bytes 204800 | tf_op jit(solution)/shard_map/all_to_all | solution.py:246
  57.4 0.3 scan.1
  57.7 8.8 %all_to_all.38 = f32[8,40,128]{2,1,0:T(8,128)S(1)} all-to-all(f32[8,40,128]{2,1,0:T(8,128)S(1)} %bitcast.21), channel_id=1, replica_groups=mesh['th'=8,'tl'=8,'sx'=4,'sy'=2] {'tl'}, dimensions={0} | all-to-all | bytes 327680 | tf_op jit(solution)/shard_map/all_to_all | solution.py:246
  66.5 0.8 final.1
  67.3 12.8 %all_to_all.39 = f32[64,4,128]{2,1,0:T(4,128)S(1)} all-to-all(f32[64,4,128]{2,1,0:T(4,128)S(1)} %bitcast.22), channel_id=1, replica_groups=mesh['th'=8,'tl'=8,'sx'=4,'sy'=2] {'tl','sx','sy'}, dimensions={0} | all-to-all | bytes 262144 | tf_op jit(solution)/shard_map/all_to_all | solution.py:246
  80.2 16.1 %all_to_all.40 = f32[8,16,128]{2,1,0:T(8,128)S(1)} all-to-all(f32[8,16,128]{2,1,0:T(8,128)S(1)} %bitcast.26), channel_id=1, replica_groups=mesh['th'=8,'tl'=8,'sx'=4,'sy'=2] {'th'}, dimensions={0} | all-to-all | bytes 131072 | tf_op jit(solution)/shard_map/all_to_all | solution.py:246
  96.3 9.6 %all_to_all.41 = f32[8,48,128]{2,1,0:T(8,128)S(1)} all-to-all(f32[8,48,128]{2,1,0:T(8,128)S(1)} %bitcast.20), channel_id=1, replica_groups=mesh['th'=8,'tl'=8,'sx'=4,'sy'=2] {'tl'}, dimensions={0} | all-to-all | bytes 393216 | tf_op jit(solution)/shard_map/all_to_all | solution.py:246
  105.9 0.8 unpack.1
  (3 shorter events, 0.1 us)

commit v13 on v9

--- a/solution.py
+++ b/solution.py
@@ -100,7 +100,7 @@
                 st_ref[pl.ds(32 * q + 2 * k + r, 8, stride=4), :] = turn[pl.ds(2 * q + r, 8, stride=16), :]
 
 
-def first_kernel(recv_ref, st_ref, out_ref, inv_ref, rhs_ref, fac_ref, scr):
+def first_kernel(recv_ref, st_ref, out_ref, rhs_ref, scr):
     d = space()
     for s in range(ND):
         scr[s] = recv_ref[s, SRC1[0] : SRC1[0] + 32, :]
@@ -113,12 +113,9 @@
         for s in range(ND):
             scr[s] = scr[s] + v[s][4:36]
 
-    inv1 = inverse(recv_ref, 1, 4, d)
     rhs = phi([scr[s] for s in range(ND)], inverse(recv_ref, 0, 8, d))
     for s in range(ND):
         react0 = recv_ref[s, REACT + 1 : REACT + 2, :]
-        inv_ref[s] = inv1[s]
-        fac_ref[s] = 1.0 / (1.0 + 2.0 * (react0 + recv_ref[s, DAMP[0] + 11 : DAMP[0] + 27, :]))
         part = rhs[s][4:28] + recv_ref[s, SRC0[0] : SRC0[0] + 24, :]
         rhs_ref[s] = part[4:20]
         out_ref[64 * s : 64 * s + 24, :] = part
@@ -165,14 +162,16 @@
         carry = carry / (1.0 + 2.0 * (react + damp)) + recv2_ref[64 * j : 64 * j + 24, :]
 
 
-def final_kernel(recv1_ref, inv_ref, rhs_ref, fac_ref, recv_ref, out_ref, layers):
+def final_kernel(recv1_ref, rhs_ref, recv_ref, out_ref, layers):
     last = is_last_slab()
     field = []
     for s in range(ND):
         incoming = recv_ref[24 * s : 24 * s + 24, :]
-        layers[0, 16 * s : 16 * s + 16, :] = fac_ref[s] * incoming[4:20] + rhs_ref[s]
+        react0 = recv1_ref[s, REACT + 1 : REACT + 2, :]
+        factor = 1.0 / (1.0 + 2.0 * (react0 + recv1_ref[s, DAMP[0] + 11 : DAMP[0] + 27, :]))
+        layers[0, 16 * s : 16 * s + 16, :] = factor * incoming[4:20] + rhs_ref[s]
         field.append(jnp.where(last, recv1_ref[s, TERM[0] + 8 : TERM[0] + 32, :], incoming))
-    w = phi(field, [inv_ref[s] for s in range(ND)])
+    w = phi(field, inverse(recv1_ref, 1, 4, space()))
     for s in range(ND):
         layers[1, 16 * s : 16 * s + 16, :] = w[s][4:20] + recv1_ref[s, SRC1[0] + 8 : SRC1[0] + 24, :]
     for s in range(ND):
@@ -251,9 +250,9 @@
         pack_kernel, [(ND, ROWS1, 128), (256, 128)], [SM, SM] + [VM] * 4, [scratch(152), scratch(128)], "pack"
     )(contact_stiff, regions, sources, damping, terminal, forward_states)
     recv1 = exchange(send1, xy)
-    send2, inv1, rhs, fac = call(
+    send2, rhs = call(
         first_kernel,
-        [(512, 128), (8, 24, 128), (8, 16, 128), (8, 16, 128)],
+        [(512, 128), (8, 16, 128)],
         [VM, VM],
         [pltpu.VMEM((8, 32, 128), F32)],
         "first",
@@ -263,8 +262,8 @@
     recv_h = exchange(send_h, "th")
     send3 = call(scan_kernel, [(192, 128)], [VM] * 3, name="scan")(recv1, recv2, recv_h)
     recv3 = exchange(send3, "tl")
-    layers = call(final_kernel, [(256, 128)], [VM] * 5, [pltpu.VMEM((2, 128, 128), F32)], "final")(
-        recv1, near(inv1), near(rhs), near(fac), recv3
+    layers = call(final_kernel, [(256, 128)], [VM] * 3, [pltpu.VMEM((2, 128, 128), F32)], "final")(
+        recv1, near(rhs), recv3
     )
     layers = exchange(layers, group, 64)
     part = call(product_kernel, [(128, 128)], [VM, VM], [scratch(32)], "product")(recv2, layers)

time: 107 us -> 107 us (level)
  no operation moved by 1% of the time
where the time goes in v13:
time: 107 us
  blocking collectives  102 us (95%)
  Pallas kernels  4.22 us (4%)
    all_to_all x7, blocking collectives, exchange(): return near(lax.all_to_all(v3, axes, 0, 0, tiled=True).reshape(v.shape))  102 us

profile of v13, /device:TPU:2, one launch (start us, length us, event | category | flops | bytes accessed | tf_op | source)
XLA Modules:
  0.0 107.0 jit_solution(10288573351855371718)
XLA Ops:
  0.6 1.3 %pack.1 = (f32[8,136,128]{2,1,0:T(8,128)S(1)}, f32[256,128]{1,0:T(8,128)S(1)}) custom-call(f32[8]{0:T(128)} %stiff_ref.1, s32[2,1,2]{2,1,0:T(1,128)} %reg_ref.1, f32[2,8,16,128]{3,2,1,0:T(8,128)} %src_ref.1, f32[8,16,128]{2,1,0:T(8,128)} %damp_ref.1, f32[8,16,128]{2,1,0:T(8,128)} %term_ref.1, f32[2,8,16,128]{3,2,1,0:T(8,128)} %state_ref.1), custom_call_target="tpu_custom_call" | custom-call | tf_op jit(solution)/shard_map/pack/pallas_call | solution.py:249
  1.9 15.0 %all_to_all.35.recv_ref.recv1_ref = f32[8,136,128]{2,1,0:T(8,128)S(1)} all-to-all(f32[8,136,128]{2,1,0:T(8,128)S(1)} %get-tuple-element.6), channel_id=1, replica_groups=mesh['th'=8,'tl'=8,'sx'=4,'sy'=2] {'sx','sy'}, dimensions={0} | all-to-all | bytes 1114112 | tf_op jit(solution)/shard_map/all_to_all | solution.py:243
  16.9 0.9 first.1
  17.8 12.2 %all_to_all.36 = f32[8,64,128]{2,1,0:T(8,128)S(1)} all-to-all(f32[8,64,128]{2,1,0:T(8,128)S(1)} %bitcast.25), channel_id=1, replica_groups=mesh['th'=8,'tl'=8,'sx'=4,'sy'=2] {'tl'}, dimensions={0} | all-to-all | bytes 524288 | tf_op jit(solution)/shard_map/all_to_all | solution.py:243
  30.1 27.8 %all_to_all.37 = f32[8,1,3200]{2,1,0:T(1,128)S(1)} all-to-all(f32[8,1,3200]{2,1,0:T(1,128)S(1)} %bitcast.20), channel_id=1, replica_groups=mesh['th'=8,'tl'=8,'sx'=4,'sy'=2] {'th'}, dimensions={0} | all-to-all | bytes 204800 | tf_op jit(solution)/shard_map/all_to_all | solution.py:243
  57.9 0.3 scan.1
  58.2 8.6 %all_to_all.38 = f32[8,24,128]{2,1,0:T(8,128)S(1)} all-to-all(f32[8,24,128]{2,1,0:T(8,128)S(1)} %bitcast.23), channel_id=1, replica_groups=mesh['th'=8,'tl'=8,'sx'=4,'sy'=2] {'tl'}, dimensions={0} | all-to-all | bytes 196608 | tf_op jit(solution)/shard_map/all_to_all | solution.py:243
  66.8 0.8 final.1
  67.6 12.6 %all_to_all.39 = f32[64,4,128]{2,1,0:T(4,128)S(1)} all-to-all(f32[64,4,128]{2,1,0:T(4,128)S(1)} %bitcast.19), channel_id=1, replica_groups=mesh['th'=8,'tl'=8,'sx'=4,'sy'=2] {'tl','sx','sy'}, dimensions={0} | all-to-all | bytes 262144 | tf_op jit(solution)/shard_map/all_to_all | solution.py:243
  80.3 16.4 %all_to_all.40 = f32[8,16,128]{2,1,0:T(8,128)S(1)} all-to-all(f32[8,16,128]{2,1,0:T(8,128)S(1)} %bitcast.24), channel_id=1, replica_groups=mesh['th'=8,'tl'=8,'sx'=4,'sy'=2] {'th'}, dimensions={0} | all-to-all | bytes 131072 | tf_op jit(solution)/shard_map/all_to_all | solution.py:243
  96.7 9.4 %all_to_all.41 = f32[8,48,128]{2,1,0:T(8,128)S(1)} all-to-all(f32[8,48,128]{2,1,0:T(8,128)S(1)} %bitcast.18), channel_id=1, replica_groups=mesh['th'=8,'tl'=8,'sx'=4,'sy'=2] {'tl'}, dimensions={0} | all-to-all | bytes 393216 | tf_op jit(solution)/shard_map/all_to_all | solution.py:243
  106.1 0.8 unpack.1
  (3 shorter events, 0.1 us)

commit v14 on v12

--- a/solution.py
+++ b/solution.py
@@ -136,7 +136,7 @@
     carry = recv_ref[41 * (NL - 1) : 41 * (NL - 1) + 24, :]
     for j in range(NL - 2, -1, -1):
         react = recv_ref[41 * j + 24 : 41 * j + 25, :]
-        carry = carry / (1.0 + 2.0 * (react + damp)) + recv_ref[41 * j : 41 * j + 24, :]
+        carry = carry * (1.0 / (1.0 + 2.0 * (react + damp))) + recv_ref[41 * j : 41 * j + 24, :]
     group = lax.broadcasted_iota(jnp.int32, (1, 128), 1) // 16
     tail = recv_ref[24:25, :]
     for j in range(1, NL):
@@ -159,12 +159,12 @@
         for j in range(NL):
             term = 1.0 + 2.0 * (react[j : j + 1] + damp)
             den = term if den is None else den * term
-        carry = jnp.where(h > me, carry / den + recv_ref[25 * h : 25 * h + 24, :], carry)
+        carry = jnp.where(h > me, carry * (1.0 / den) + recv_ref[25 * h : 25 * h + 24, :], carry)
     for j in range(NL - 1, -1, -1):
         out_ref[40 * j : 40 * j + 24, :] = carry
         out_ref[40 * j + 24 : 40 * j + 40, :] = st_ref[128 + 16 * j : 144 + 16 * j, :]
         react = recv2_ref[41 * j + 24 : 41 * j + 25, :]
-        carry = carry / (1.0 + 2.0 * (react + damp)) + recv2_ref[41 * j : 41 * j + 24, :]
+        carry = carry * (1.0 / (1.0 + 2.0 * (react + damp))) + recv2_ref[41 * j : 41 * j + 24, :]
 
 
 def final_kernel(recv1_ref, inv_ref, rhs_ref, fac_ref, recv_ref, out_ref, layers):

time: 107 us -> 107 us (level)
  no operation moved by 1% of the time
where the time goes in v14:
time: 107 us
  blocking collectives  102 us (95%)
  Pallas kernels  4.22 us (4%)
    all_to_all x7, blocking collectives, exchange(): return near(lax.all_to_all(v3, axes, 0, 0, tiled=True).reshape(v.shape))  102 us

profile of v14, /device:TPU:2, one launch (start us, length us, event | category | flops | bytes accessed | tf_op | source)
XLA Modules:
  0.0 106.7 jit_solution(6430040292969513918)
XLA Ops:
  0.6 1.3 %pack.1 = (f32[8,136,128]{2,1,0:T(8,128)S(1)}, f32[256,128]{1,0:T(8,128)S(1)}) custom-call(f32[8]{0:T(128)} %stiff_ref.1, s32[2,1,2]{2,1,0:T(1,128)} %reg_ref.1, f32[2,8,16,128]{3,2,1,0:T(8,128)} %src_ref.1, f32[8,16,128]{2,1,0:T(8,128)} %damp_ref.1, f32[8,16,128]{2,1,0:T(8,128)} %term_ref.1, f32[2,8,16,128]{3,2,1,0:T(8,128)} %state_ref.1), custom_call_target="tpu_custom_call" | custom-call | tf_op jit(solution)/shard_map/pack/pallas_call | solution.py:252
  1.9 15.0 %all_to_all.35.recv_ref.recv1_ref = f32[8,136,128]{2,1,0:T(8,128)S(1)} all-to-all(f32[8,136,128]{2,1,0:T(8,128)S(1)} %get-tuple-element.8), channel_id=1, replica_groups=mesh['th'=8,'tl'=8,'sx'=4,'sy'=2] {'sx','sy'}, dimensions={0} | all-to-all | bytes 1114112 | tf_op jit(solution)/shard_map/all_to_all | solution.py:246
  16.9 0.9 first.1
  17.8 11.6 %all_to_all.36 = f32[8,1,5248]{2,1,0:T(1,128)S(1)} all-to-all(f32[8,1,5248]{2,1,0:T(1,128)S(1)} %bitcast.27), channel_id=1, replica_groups=mesh['th'=8,'tl'=8,'sx'=4,'sy'=2] {'tl'}, dimensions={0} | all-to-all | bytes 335872 | tf_op jit(solution)/shard_map/all_to_all | solution.py:246
  29.4 27.9 %all_to_all.37 = f32[8,1,3200]{2,1,0:T(1,128)S(1)} all-to-all(f32[8,1,3200]{2,1,0:T(1,128)S(1)} %bitcast.24), channel_id=1, replica_groups=mesh['th'=8,'tl'=8,'sx'=4,'sy'=2] {'th'}, dimensions={0} | all-to-all | bytes 204800 | tf_op jit(solution)/shard_map/all_to_all | solution.py:246
  57.4 0.3 scan.1
  57.7 8.8 %all_to_all.38 = f32[8,40,128]{2,1,0:T(8,128)S(1)} all-to-all(f32[8,40,128]{2,1,0:T(8,128)S(1)} %bitcast.21), channel_id=1, replica_groups=mesh['th'=8,'tl'=8,'sx'=4,'sy'=2] {'tl'}, dimensions={0} | all-to-all | bytes 327680 | tf_op jit(solution)/shard_map/all_to_all | solution.py:246
  66.5 0.8 final.1
  67.3 12.8 %all_to_all.39 = f32[64,4,128]{2,1,0:T(4,128)S(1)} all-to-all(f32[64,4,128]{2,1,0:T(4,128)S(1)} %bitcast.22), channel_id=1, replica_groups=mesh['th'=8,'tl'=8,'sx'=4,'sy'=2] {'tl','sx','sy'}, dimensions={0} | all-to-all | bytes 262144 | tf_op jit(solution)/shard_map/all_to_all | solution.py:246
  80.2 16.1 %all_to_all.40 = f32[8,16,128]{2,1,0:T(8,128)S(1)} all-to-all(f32[8,16,128]{2,1,0:T(8,128)S(1)} %bitcast.26), channel_id=1, replica_groups=mesh['th'=8,'tl'=8,'sx'=4,'sy'=2] {'th'}, dimensions={0} | all-to-all | bytes 131072 | tf_op jit(solution)/shard_map/all_to_all | solution.py:246
  96.3 9.6 %all_to_all.41 = f32[8,48,128]{2,1,0:T(8,128)S(1)} all-to-all(f32[8,48,128]{2,1,0:T(8,128)S(1)} %bitcast.20), channel_id=1, replica_groups=mesh['th'=8,'tl'=8,'sx'=4,'sy'=2] {'tl'}, dimensions={0} | all-to-all | bytes 393216 | tf_op jit(solution)/shard_map/all_to_all | solution.py:246
  105.9 0.8 unpack.1
  (3 shorter events, 0.1 us)
